TPU v7x, 128 devices: a whole 4x4x4 slice. The times are simulated.
128 devices in a mesh: tok: 16 (over y, z), head: 8 (over x, core).
Axes of the slice: x: 4, y: 4, z: 4, core: 2. Of those that a mesh axis runs over, the one named last changes fastest.
Arguments:
- prefill_states: bfloat16 [4, 2048, 2048], P(None, 'tok'), may hold values from -6 to 6
- decode_states: bfloat16 [128, 2048], P('tok'), may hold values from -6 to 6
- attn_gain: float32 [2048], replicated, may hold values from 0.1 to 1.9
- w_qkv: bfloat16 [2048, 3, 2048], P(None, None, 'head'), may hold values from -0.125 to 0.125
- w_out: bfloat16 [2048, 2048], P('head'), may hold values from -0.125 to 0.125
- ffn_gain: float32 [2048], replicated, may hold values from 0.1 to 1.9
- w_gate_up: bfloat16 [2048, 2, 5120], P(None, None, 'tok'), may hold values from -0.125 to 0.125
- w_down: bfloat16 [5120, 2048], P('tok'), may hold values from -0.078125 to 0.078125
- prefill_pool: bfloat16 [768, 128, 1024], P('tok', None, 'head')
- prefill_pages: int32 [16, 48], P('tok'), may hold values from 0 to 47, as said below
- prefill_lengths: int32 [4], replicated, may hold values from 1 to 6144, as said below
- prefill_home: int32 [16], replicated, may hold values from 0 to 15, each once
- decode_pool: bfloat16 [1024, 128, 4096], P('tok', None, 'head')
- decode_pages: int32 [128, 32], P('tok'), may hold values from 0 to 63, as said below
- decode_lengths: int32 [128], P('tok'), may hold values from 1 to 4096, as said below
- decode_home: int32 [128], replicated, may hold values from 0 to 127, each once
Outputs:
- prefill_out: bfloat16 [4, 2048, 2048], P(None, ('tok', 'head'))
- decode_out: bfloat16 [128, 2048], P(('tok', 'head'))
Inputs may be any that keep to these rules, and one draw needn't show every extreme that they name: `prefill_pages`: each row is an ordering of all 48 pages of the prefill pool on that row's tok index. `prefill_lengths`: one prefill request has exactly 6144 cached tokens. `decode_pages`: slot s lies on tok index s // 8; within one tok index the first ceil(length / 128) pages of its slots are all different. `decode_lengths`: every tok index hosts one decode request of exactly 4096 cached tokens.
All inputs are finite; a program needn't handle non-finite values.
Results may differ from a plain program's by a relative error of at most 0.017.
The roundings to bfloat16 on the way count: a program that leaves them out, or rounds other values in their place, can miss the bound.
Values may be sent and summed in bfloat16 or wider, within the bound.
A program may use at most 128 MiB of HBM per device.

v0:
```python
import math

import jax
import jax.numpy as jnp
from jax import lax
from jax.sharding import PartitionSpec as P

HD = 64


EPSILON = 1e-06
SCALE = 0.125
MASKED = -1e30


def rms_norm(rows, gain):
    values = rows.astype(jnp.float32)
    inverse = lax.rsqrt(jnp.mean(values * values, axis=-1, keepdims=True) + EPSILON)
    return (values * inverse * gain).astype(jnp.bfloat16)


def inner(left, right):
    return lax.dot_general(
        left, right, (((1,), (1,)), ((), ())), preferred_element_type=jnp.float32
    )


def shards(
    prefill_states,
    decode_states,
    attn_gain,
    w_qkv,
    w_out,
    ffn_gain,
    w_gate_up,
    w_down,
    prefill_pool,
    prefill_pages,
    prefill_lengths,
    prefill_home,
    decode_pool,
    decode_pages,
    decode_lengths,
    decode_home,
):
    n_tok = lax.axis_size("tok")
    n_head = lax.axis_size("head")
    my_tok = lax.axis_index("tok")
    my_head = lax.axis_index("head")
    requests, positions, width = prefill_states.shape
    hosted = decode_states.shape[0]
    heads_per = w_qkv.shape[2] // HD
    stretch = positions * n_tok
    units = requests * heads_per
    features = heads_per * HD
    normed_pre = rms_norm(prefill_states, attn_gain).reshape(requests * positions, width)
    normed_dec = rms_norm(decode_states, attn_gain)
    normed = jnp.concatenate([normed_pre, normed_dec], axis=0)
    projected = jnp.dot(
        normed, w_qkv.reshape(width, 3 * features), preferred_element_type=jnp.float32
    ).astype(jnp.bfloat16)
    proj_pre = projected[: requests * positions].reshape(requests, positions, 3, heads_per, HD)
    proj_dec = projected[requests * positions :]
    unit_ids = jnp.arange(units, dtype=jnp.int32)
    host_ids = jnp.arange(n_tok, dtype=jnp.int32)
    hosted_unit = jnp.sum(
        jnp.where(prefill_home[None, :] == host_ids[:, None], unit_ids[None, :], 0), axis=1
    )
    by_unit = jnp.transpose(proj_pre, (0, 3, 1, 2, 4)).reshape(units, positions * 3 * HD)
    outgoing = jnp.take(by_unit, hosted_unit, axis=0)
    pre_cols = positions * 3 * HD
    spread = jnp.broadcast_to(
        proj_dec.reshape(1, hosted * 3 * features), (n_tok, hosted * 3 * features)
    )
    outgoing = jnp.concatenate([outgoing, spread], axis=1)
    arrived = lax.all_to_all(outgoing, "tok", split_axis=0, concat_axis=0, tiled=True)
    arrived_dec = arrived[:, pre_cols:].reshape(n_tok * hosted, 3, heads_per, HD)
    arrived_pre = arrived[:, :pre_cols].reshape(stretch, 3, HD)
    query_rows = arrived_pre[:, 0]
    key_rows = arrived_pre[:, 1]
    value_rows = arrived_pre[:, 2]
    my_unit = hosted_unit[my_tok]
    length = prefill_lengths[my_unit // heads_per]
    cache = jnp.take(prefill_pool, prefill_pages[0], axis=0).reshape(-1, 2 * HD)
    cache_keys = cache[:, :HD]
    cache_values = cache[:, HD:]
    span = cache.shape[0]
    block = math.gcd(stretch, 512)

    def attend(start):
        rows = lax.dynamic_slice_in_dim(query_rows, start, block, 0)
        score_cache = inner(rows, cache_keys) * SCALE
        score_cache = jnp.where(jnp.arange(span)[None, :] < length, score_cache, MASKED)
        score_stretch = inner(rows, key_rows) * SCALE
        row_pos = start + jnp.arange(block)[:, None]
        score_stretch = jnp.where(jnp.arange(stretch)[None, :] <= row_pos, score_stretch, MASKED)
        top = jnp.maximum(
            jnp.max(score_cache, axis=1, keepdims=True),
            jnp.max(score_stretch, axis=1, keepdims=True),
        )
        weight_cache = jnp.exp(score_cache - top)
        weight_stretch = jnp.exp(score_stretch - top)
        total = jnp.sum(weight_cache, axis=1, keepdims=True) + jnp.sum(
            weight_stretch, axis=1, keepdims=True
        )
        mixed = jnp.dot(
            weight_cache.astype(jnp.bfloat16), cache_values, preferred_element_type=jnp.float32
        )
        mixed = mixed + jnp.dot(
            weight_stretch.astype(jnp.bfloat16), value_rows, preferred_element_type=jnp.float32
        )
        return (mixed / total).astype(jnp.bfloat16)

    starts = jnp.arange(stretch // block, dtype=jnp.int32) * block
    attn_unit = lax.map(attend, starts).reshape(stretch, HD)
    slots = my_tok * hosted + jnp.arange(hosted, dtype=jnp.int32)
    all_requests = jnp.arange(decode_home.shape[0], dtype=jnp.int32)
    anchor = jnp.sum(
        jnp.where(decode_home[None, :] == slots[:, None], all_requests[None, :], 0), axis=1
    )
    mine = jnp.take(arrived_dec, anchor, axis=0)

    def decode_one(operands):
        pages, slot_length, rows = operands
        cache_slot = jnp.take(decode_pool, pages, axis=0).reshape(-1, heads_per, 2 * HD)
        query = rows[0]
        scores = (
            jnp.einsum(
                "hd,khd->hk", query, cache_slot[:, :, :HD], preferred_element_type=jnp.float32
            )
            * SCALE
        )
        scores = jnp.where(jnp.arange(cache_slot.shape[0])[None, :] < slot_length, scores, MASKED)
        own_score = (
            jnp.sum(query.astype(jnp.float32) * rows[1].astype(jnp.float32), axis=1, keepdims=True)
            * SCALE
        )
        top = jnp.maximum(jnp.max(scores, axis=1, keepdims=True), own_score)
        weights = jnp.exp(scores - top)
        own_weight = jnp.exp(own_score - top)
        total = jnp.sum(weights, axis=1, keepdims=True) + own_weight
        mixed = jnp.einsum(
            "hk,khd->hd",
            weights.astype(jnp.bfloat16),
            cache_slot[:, :, HD:],
            preferred_element_type=jnp.float32,
        )
        mixed = mixed + own_weight.astype(jnp.bfloat16).astype(jnp.float32) * rows[2].astype(
            jnp.float32
        )
        return (mixed / total).astype(jnp.bfloat16).reshape(features)

    decode_attn = lax.map(decode_one, (decode_pages, decode_lengths, mine))
    backward = attn_unit.reshape(n_tok, positions * HD)
    back_cols = positions * HD
    spread_back = jnp.broadcast_to(
        decode_attn.reshape(1, hosted * features), (n_tok, hosted * features)
    )
    backward = jnp.concatenate([backward, spread_back], axis=1)
    returned = lax.all_to_all(backward, "tok", split_axis=0, concat_axis=0, tiled=True)
    by_slot = returned[:, back_cols:].reshape(n_tok * hosted, features)
    my_slots = lax.dynamic_slice_in_dim(decode_home, my_tok * hosted, hosted, 0)
    attn_dec = jnp.take(by_slot, my_slots, axis=0)
    attn_pre = jnp.take(returned[:, :back_cols], prefill_home, axis=0).reshape(
        requests, heads_per, positions, HD
    )
    block_rows = positions // n_head
    decode_share = hosted // n_head
    per = requests * block_rows + decode_share
    pre_rows = jnp.transpose(attn_pre, (0, 2, 1, 3)).reshape(requests, n_head, block_rows, features)
    pre_rows = jnp.transpose(pre_rows, (1, 0, 2, 3)).reshape(
        n_head, requests * block_rows, features
    )
    dec_rows = attn_dec.reshape(n_head, decode_share, features)
    ordered = jnp.concatenate([pre_rows, dec_rows], axis=1).reshape(n_head * per, features)
    mixed_rows = lax.psum_scatter(
        jnp.dot(ordered, w_out, preferred_element_type=jnp.float32).astype(jnp.bfloat16),
        "head",
        scatter_dimension=0,
        tiled=True,
    ).astype(jnp.float32)
    own_pre = lax.dynamic_slice_in_dim(prefill_states, my_head * block_rows, block_rows, 1).reshape(
        requests * block_rows, width
    )
    own_dec = lax.dynamic_slice_in_dim(decode_states, my_head * decode_share, decode_share, 0)
    resid = jnp.concatenate([own_pre, own_dec], axis=0).astype(jnp.float32) + mixed_rows
    normed_mid = rms_norm(resid, ffn_gain)
    piece = lax.all_gather(normed_mid, "tok", axis=0, tiled=True)
    gate = jnp.dot(piece, w_gate_up[:, 0], preferred_element_type=jnp.float32)
    upper = jnp.dot(piece, w_gate_up[:, 1], preferred_element_type=jnp.float32)
    hidden = (jax.nn.gelu(gate, approximate=True) * upper).astype(jnp.bfloat16)
    summed = lax.psum(
        jnp.dot(hidden, w_down, preferred_element_type=jnp.float32).astype(jnp.bfloat16), "tok"
    ).astype(jnp.float32)
    ffn_rows = lax.dynamic_slice_in_dim(summed, my_tok * per, per, 0)
    result = (resid + ffn_rows).astype(jnp.bfloat16)
    prefill_out = result[: requests * block_rows].reshape(requests, block_rows, width)
    decode_out = result[requests * block_rows :]
    return (prefill_out, decode_out)


def solution(mesh):
    placed = (
        P(None, "tok", None),
        P("tok", None),
        P(),
        P(None, None, "head"),
        P("head", None),
        P(),
        P(None, None, "tok"),
        P("tok", None),
        P("tok", None, "head"),
        P("tok", None),
        P(),
        P(),
        P("tok", None, "head"),
        P("tok", None),
        P("tok"),
        P(),
    )
    return jax.shard_map(
        shards,
        mesh=mesh,
        in_specs=placed,
        out_specs=(P(None, ("tok", "head"), None), P(("tok", "head"), None)),
        check_vma=False,
    )
```

profile of v0, /device:TPU:0, one launch (start us, length us, event | category | flops | bytes accessed | tf_op | source)
XLA Modules:
  0.0 700.5 jit_solution(3987301994790291985)
XLA Ops:
  36.3 8.7 %all-to-all-start = ((bf16[16,2,15360]{2,1,0:T(2,128)(2,1)}), bf16[16,2,15360]{2,1,0:T(2,128)(2,1)}, u32[]{:S(2)}, u32[]{:S(2)}) async-start(bf16[16,2,15360]{2,1,0:T(2,128)(2,1)} %reshape.373), calls=%async_computation | async-start | bytes 1966080 | tf_op jit(solution)/shard_map/all_to_all | solution.py:76
  67.8 310.7 %while.21 = (s32[]{:T(128)}, bf16[8,256]{1,0:T(8,128)(2,1)S(1)}, s32[8]{0:T(128)S(1)}, bf16[8,3,4,64]{3,2,1,0:T(4,128)(2,1)S(1)}, s32[8,32]{1,0:T(8,128)}, /*ind...) while((s32[]{:T(128)}, bf16[8,256]{1,0:T(8,128)(2,1)S(1)}, s32[8]{0:T(128)S(1)}, ...), condition=%wide.region_14.15_spmd, body=%wide.region_10.14_spmd.sunk | while | flops 6430264 | bytes 38044244 | solution.py:153
  76.9 6.9 gather.55
  83.8 16.5 %broadcast_select_fusion.4 = bf16[4096,4,128]{2,1,0:T(4,128)(2,1)S(1)} fusion(bf16[4096,4,128]{2,1,0:T(4,128)(2,1)} %gather.55, pred[4096]{0:T(1024)(128)(4,1)S(1)} %broadcast_bitcast_fusion.3), kind=kLoop, calls=%fused_computation.38.clone.1 | loop fusion | flops 2097152 | bytes 8392704 | tf_op jit(solution)/shard_map/while/body/eval_jaxpr/jit(_take)/select_n | solution.py:125
  115.7 6.9 gather.55
  122.6 16.5 %broadcast_select_fusion.4 = bf16[4096,4,128]{2,1,0:T(4,128)(2,1)S(1)} fusion(bf16[4096,4,128]{2,1,0:T(4,128)(2,1)} %gather.55, pred[4096]{0:T(1024)(128)(4,1)S(1)} %broadcast_bitcast_fusion.3), kind=kLoop, calls=%fused_computation.38.clone.1 | loop fusion | flops 2097152 | bytes 8392704 | tf_op jit(solution)/shard_map/while/body/eval_jaxpr/jit(_take)/select_n | solution.py:125
  154.6 6.9 gather.55
  161.5 16.5 %broadcast_select_fusion.4 = bf16[4096,4,128]{2,1,0:T(4,128)(2,1)S(1)} fusion(bf16[4096,4,128]{2,1,0:T(4,128)(2,1)} %gather.55, pred[4096]{0:T(1024)(128)(4,1)S(1)} %broadcast_bitcast_fusion.3), kind=kLoop, calls=%fused_computation.38.clone.1 | loop fusion | flops 2097152 | bytes 8392704 | tf_op jit(solution)/shard_map/while/body/eval_jaxpr/jit(_take)/select_n | solution.py:125
  193.4 6.9 gather.55
  200.3 16.5 %broadcast_select_fusion.4 = bf16[4096,4,128]{2,1,0:T(4,128)(2,1)S(1)} fusion(bf16[4096,4,128]{2,1,0:T(4,128)(2,1)} %gather.55, pred[4096]{0:T(1024)(128)(4,1)S(1)} %broadcast_bitcast_fusion.3), kind=kLoop, calls=%fused_computation.38.clone.1 | loop fusion | flops 2097152 | bytes 8392704 | tf_op jit(solution)/shard_map/while/body/eval_jaxpr/jit(_take)/select_n | solution.py:125
  232.2 6.9 gather.55
  239.1 16.5 %broadcast_select_fusion.4 = bf16[4096,4,128]{2,1,0:T(4,128)(2,1)S(1)} fusion(bf16[4096,4,128]{2,1,0:T(4,128)(2,1)} %gather.55, pred[4096]{0:T(1024)(128)(4,1)S(1)} %broadcast_bitcast_fusion.3), kind=kLoop, calls=%fused_computation.38.clone.1 | loop fusion | flops 2097152 | bytes 8392704 | tf_op jit(solution)/shard_map/while/body/eval_jaxpr/jit(_take)/select_n | solution.py:125
  271.1 6.9 gather.55
  278.0 16.5 %broadcast_select_fusion.4 = bf16[4096,4,128]{2,1,0:T(4,128)(2,1)S(1)} fusion(bf16[4096,4,128]{2,1,0:T(4,128)(2,1)} %gather.55, pred[4096]{0:T(1024)(128)(4,1)S(1)} %broadcast_bitcast_fusion.3), kind=kLoop, calls=%fused_computation.38.clone.1 | loop fusion | flops 2097152 | bytes 8392704 | tf_op jit(solution)/shard_map/while/body/eval_jaxpr/jit(_take)/select_n | solution.py:125
  309.9 6.9 gather.55
  316.8 16.5 %broadcast_select_fusion.4 = bf16[4096,4,128]{2,1,0:T(4,128)(2,1)S(1)} fusion(bf16[4096,4,128]{2,1,0:T(4,128)(2,1)} %gather.55, pred[4096]{0:T(1024)(128)(4,1)S(1)} %broadcast_bitcast_fusion.3), kind=kLoop, calls=%fused_computation.38.clone.1 | loop fusion | flops 2097152 | bytes 8392704 | tf_op jit(solution)/shard_map/while/body/eval_jaxpr/jit(_take)/select_n | solution.py:125
  348.7 6.9 gather.55
  355.6 16.5 %broadcast_select_fusion.4 = bf16[4096,4,128]{2,1,0:T(4,128)(2,1)S(1)} fusion(bf16[4096,4,128]{2,1,0:T(4,128)(2,1)} %gather.55, pred[4096]{0:T(1024)(128)(4,1)S(1)} %broadcast_bitcast_fusion.3), kind=kLoop, calls=%fused_computation.38.clone.1 | loop fusion | flops 2097152 | bytes 8392704 | tf_op jit(solution)/shard_map/while/body/eval_jaxpr/jit(_take)/select_n | solution.py:125
  384.3 76.3 %while.20 = (s32[]{:T(128)}, bf16[4,512,64]{1,2,0:T(8,128)(2,1)}, s32[]{:T(128)}, s32[4]{0:T(128)}, bf16[2048,64]{1,0:T(8,128)(2,1)S(1)}, /*index=5*/bf16[6144,6...) while((s32[]{:T(128)}, bf16[4,512,64]{1,2,0:T(8,128)(2,1)}, ...), condition=%wide.region_8.9_spmd, body=%wide.region_3.8_spmd.sunk | while | flops 1116837376 | bytes 57026836 | solution.py:115
  473.1 7.1 %all-to-all-done.1 = bf16[16,2,5120]{2,1,0:T(2,128)(2,1)S(1)} async-done(((bf16[16,2,5120]{2,1,0:T(2,128)(2,1)}), bf16[16,2,5120]{2,1,0:T(2,128)(2,1)S(1)}, u32[]{:S(2)}, u32[]{:S(2)}) %all-to-all-start.1) | async-done | bytes 327712 | tf_op jit(solution)/shard_map/all_to_all | solution.py:160
  486.1 23.3 %fusion = bf16[72,2048]{1,0:T(8,128)(2,1)S(1)} fusion(bf16[520,2048]{1,0:T(8,128)(2,1)S(1)} %convolution_convert_fusion.1), kind=kCustom, calls=%all-reduce-scatter | all-reduce-scatter fusion | flops 1179649 | bytes 2425344
  513.6 53.0 %all-gather.3.cloned.1.call-done = bf16[16,65,2048]{2,1,0:T(8,128)(2,1)} async-done(((bf16[1,65,2048]{2,1,0:T(8,128)(2,1)}), bf16[16,65,2048]{2,1,0:T(8,128)(2,1)}) %all-gather.3.cloned.1.call-update) | async-done | bytes 4259856 | tf_op jit(solution)/shard_map/all_gather | solution.py:188
  576.7 10.4 %convolution_convert_fusion = bf16[1040,2048]{1,0:T(8,128)(2,1)} fusion(bf16[320,2048]{1,0:T(8,128)(2,1)} %param.27, bf16[1040,2048]{1,0:T(8,128)(2,1)} %reshape.365, f32[1040,320]{0,1:T(8,128)} %fusion.71, bf16[2048,2,320]{0,2,1:T(8,128)(2,1)} %param.26), kind=kOutput, calls=%fused_computation.70 | convolution fusion | flops 2731755520 | bytes 12615680 | tf_op jit(solution)/shard_map/dot_general | solution.py:193
  587.1 103.8 %all-reduce.4.cloned.1.call-done = bf16[1040,2048]{1,0:T(8,128)(2,1)} async-done(((bf16[1040,2048]{1,0:T(8,128)(2,1)}), bf16[1040,2048]{1,0:T(8,128)(2,1)}) %all-reduce.4.cloned.1.call-update) | async-done | bytes 4259856 | tf_op jit(solution)/shard_map/psum | solution.py:192
  (344 shorter events, 281.1 us)
Async XLA Ops:
  7.2 47.6 %copy-start = (bf16[48,128,128]{2,1,0:T(8,128)(2,1)S(1)}, bf16[48,128,128]{2,1,0:T(8,128)(2,1)}, u32[]{:S(2)}) copy-start(bf16[48,128,128]{2,1,0:T(8,128)(2,1)} %param.28) | copy-start | bytes 4718596
  8.1 12.7 %copy-start.11 = (s32[16]{0:T(128)}, s32[16]{0:T(128)S(1)}, u32[]{:S(2)}) copy-start(s32[16]{0:T(128)S(1)} %select_reduce_fusion) | copy-start | bytes 196
  32.4 16.7 %copy-start.9 = (s32[16]{0:T(128)S(1)}, s32[16]{0:T(128)}, u32[]{:S(2)}) copy-start(s32[16]{0:T(128)} %param.31) | copy-start | bytes 196
  32.4 17.8 %copy-start.10 = (s32[128]{0:T(128)S(1)}, s32[128]{0:T(128)}, u32[]{:S(2)}) copy-start(s32[128]{0:T(128)} %param.35) | copy-start | bytes 1540
  32.5 20.0 %copy-start.8 = (u32[128]{0:T(128)S(1)}, u32[128]{0:T(128)}, u32[]{:S(2)}) copy-start(u32[128]{0:T(128)} %constant.188) | copy-start | bytes 1540
  36.3 25.6 %all-to-all-start = ((bf16[16,2,15360]{2,1,0:T(2,128)(2,1)}), bf16[16,2,15360]{2,1,0:T(2,128)(2,1)}, u32[]{:S(2)}, u32[]{:S(2)}) async-start(bf16[16,2,15360]{2,1,0:T(2,128)(2,1)} %reshape.373), calls=%async_computation | async-start | bytes 1966080 | tf_op jit(solution)/shard_map/all_to_all | solution.py:76
  61.2 6.6 copy-start.12
  387.7 3.3 copy-start.2
  397.6 4.3 copy-start.3
  397.6 4.3 copy-start.4
  416.7 4.3 copy-start.3
  416.7 4.3 copy-start.4
  435.7 4.3 copy-start.3
  435.7 4.3 copy-start.4
  454.7 4.3 copy-start.3
  454.7 4.3 copy-start.4
  460.6 21.0 %copy-start.6 = (pred[8]{0:T(512)(128)(4,1)S(1)}, pred[8]{0:T(512)(128)(4,1)}, u32[]{:S(2)}) copy-start(pred[8]{0:T(512)(128)(4,1)} %get-tuple-element.149) | copy-start | bytes 28
  463.1 20.0 %copy-start.7 = (pred[4,4]{1,0:T(4,128)(4,1)S(1)}, pred[4,4]{1,0:T(4,128)(4,1)}, u32[]{:S(2)}) copy-start(pred[4,4]{1,0:T(4,128)(4,1)} %broadcast_in_dim.177) | copy-start | bytes 52
  464.9 15.4 %all-to-all-start.1 = ((bf16[16,2,5120]{2,1,0:T(2,128)(2,1)}), bf16[16,2,5120]{2,1,0:T(2,128)(2,1)S(1)}, u32[]{:S(2)}, u32[]{:S(2)}) async-start(bf16[16,2,5120]{2,1,0:T(2,128)(2,1)} %reshape.375), calls=%async_computation.1 | async-start | bytes 655360 | tf_op jit(solution)/shard_map/all_to_all | solution.py:160
  471.5 95.1 %all-gather.3.cloned.1.call-start = ((), (), s32[]{:S(2)}) async-start(), calls=%async_computation.3 | async-start | bytes 5013504 | tf_op jit(solution)/shard_map/all_gather | solution.py:188
  484.2 28.5 %copy-start.5 = (f32[2048]{0:T(1024)S(1)}, f32[2048]{0:T(1024)}, u32[]{:S(2)}) copy-start(f32[2048]{0:T(1024)} %param.25) | copy-start | bytes 24580
  509.5 2.4 collective-permute-start
  513.6 177.4 %all-reduce.4.cloned.1.call-start = ((), (), s32[]{:S(2)}) async-start(), calls=%async_computation.2 | async-start | bytes 8519680 | tf_op jit(solution)/shard_map/psum | solution.py:192
  576.7 116.8 %copy-start.1 = (bf16[48,128,128]{2,1,0:T(8,128)(2,1)S(1)}, bf16[48,128,128]{2,1,0:T(8,128)(2,1)}, u32[]{:S(2)}) copy-start(bf16[48,128,128]{2,1,0:T(8,128)(2,1)} %param.28) | copy-start | bytes 4718596
  (3 other events, 10.0 us)
Sparse Core Ops, SparseCore 0:
  513.7 52.8 all-gather.2
  587.2 103.6 all-reduce.3
where the time goes:
time: 710 us; the launch traced here: 701 us
  other arithmetic  200 us (28%)
  local copies, waits for them, and re-layouts  193 us (27%)
  waiting for transfers between devices  165 us (23%)
  matrix products  76.3 us (11%)
  blocking collectives  23.3 us (3%)
  between operations  17.5 us (2%)
  starting transfers between devices  16.6 us (2%)
  loops' own time  8.49 us (1%)
    select_n x16, other arithmetic, decode_one(): jnp.take(decode_pool, pages, axis=0).reshape(-1, heads_per, 2 * HD)  137 us
    gather x16, local copies, waits for them, and re-layouts, decode_one(): jnp.take(decode_pool, pages, axis=0).reshape(-1, heads_per, 2 * HD)  104 us
    psum x1, waiting for transfers between devices, shards(): lax.psum(jnp.dot(hidden, w_down, preferred_element_type=jnp.float32).asty...  104 us
    all_gather x1, waiting for transfers between devices, shards(): piece = lax.all_gather(normed_mid, 'tok', axis=0, tiled=True)  53 us
    slice x8, local copies, waits for them, and re-layouts, decode_one(): cache_slot[:, :, :HD]  30.5 us
    unnamed x1, blocking collectives  23.3 us
    unnamed x32, local copies, waits for them, and re-layouts  18.4 us
    dot_general x4, matrix products, attend(): jnp.dot(weight_cache.astype(jnp.bfloat16), cache_values, preferred_elemen...  17.3 us
  transfers between devices with their start and end apart: 5, of which 5 were waited for; matrix products, arithmetic and copies ran while one was open for 2% of the time, Pallas kernels for 0%

commit v1 on v0

v1 whole, which is shorter than its diff:
```python
import math

import jax
import jax.numpy as jnp
from jax import lax
from jax.experimental import pallas as pl
from jax.experimental.pallas import tpu as pltpu
from jax.sharding import PartitionSpec as P

HD = 64
EPSILON = 1e-06
SCALE = 0.125
MASKED = -1e30
PAGE = 128
F32 = jnp.float32
BF16 = jnp.bfloat16


def rms_norm(rows, gain):
    values = rows.astype(F32)
    inverse = lax.rsqrt(jnp.mean(values * values, axis=-1, keepdims=True) + EPSILON)
    return (values * inverse * gain).astype(BF16)


def dot_nt(left, right):
    return lax.dot_general(left, right, (((1,), (1,)), ((), ())), preferred_element_type=F32)


QB = 512
KC = 512


def attention_kernel(
    pages,
    length_ref,
    dpages,
    dlens,
    qkv_ref,
    mine_ref,
    pool_ref,
    dpool_hbm,
    out_ref,
    dout_ref,
    keys,
    vals,
    query,
    score,
    top_run,
    top,
    acc,
    dpool,
    dbias,
    dscore,
    count,
    owner,
    dcount,
    sem,
):
    stretch = qkv_ref.shape[0]
    span = pool_ref.shape[0]
    npages = span // PAGE
    dspan = dpool_hbm.shape[0]
    dnpages = dspan // PAGE
    slots, dmax = dpages.shape
    copy = pltpu.make_async_copy(dpool_hbm, dpool, sem)
    copy.start()

    length = length_ref[0]

    def count_page(i, _):
        count[pages[0, i]] = jnp.clip(length - i * PAGE, 0, PAGE)
        return 0

    lax.fori_loop(0, npages, count_page, 0)

    def zero_page(i, _):
        dcount[i] = 0
        owner[i] = 0
        return 0

    lax.fori_loop(0, dnpages, zero_page, 0)
    for s in range(slots):
        used = (dlens[s] + PAGE - 1) // PAGE

        def own_page(i, _):
            page = dpages[s, i]
            owner[page] = s
            dcount[page] = jnp.minimum(dlens[s] - i * PAGE, PAGE)
            return 0

        lax.fori_loop(0, used, own_page, 0)

    lane = lax.broadcasted_iota(jnp.int32, (PAGE, PAGE), 1)
    row = lax.broadcasted_iota(jnp.int32, (PAGE, PAGE), 0)

    def fill_cached(i, _):
        where_at = pl.ds(pl.multiple_of(i * PAGE, PAGE), PAGE)
        page = pool_ref[where_at, :].astype(F32)
        bias = jnp.where((lane == HD) & (row >= count[i]), MASKED, 0.0)
        keys[where_at, :] = jnp.where(lane < HD, page, bias).astype(BF16)
        vals[where_at, :] = jnp.where(lane < HD, 1.0, page).astype(BF16)
        return 0

    lax.fori_loop(0, npages, fill_cached, 0)

    def fill_own(i, _):
        source = pl.ds(pl.multiple_of(i * PAGE, PAGE), PAGE)
        target = pl.ds(pl.multiple_of(span + i * PAGE, PAGE), PAGE)
        left = qkv_ref[source, :PAGE].astype(F32)
        right = qkv_ref[source, PAGE:].astype(F32)
        query[source, :] = jnp.where(
            lane < HD, left * SCALE, jnp.where(lane == HD, 1.0, 0.0)
        ).astype(BF16)
        keys[target, :] = jnp.where(lane < HD, pltpu.roll(left, HD, 1), 0.0).astype(BF16)
        vals[target, :] = jnp.where(lane < HD, 1.0, pltpu.roll(right, HD, 1)).astype(BF16)
        return 0

    lax.fori_loop(0, stretch // PAGE, fill_own, 0)

    def fold(s):
        best = s[:, :PAGE]
        for j in range(1, s.shape[1] // PAGE):
            best = jnp.maximum(best, s[:, j * PAGE : (j + 1) * PAGE])
        return best

    def make_scores(i, c, diagonal):
        rows = query[i * QB : (i + 1) * QB, :]
        s = dot_nt(rows, keys[pl.ds(pl.multiple_of(c * KC, KC), KC), :])
        if diagonal:
            r = lax.broadcasted_iota(jnp.int32, (QB, KC), 0)
            k = lax.broadcasted_iota(jnp.int32, (QB, KC), 1)
            s = jnp.where(k <= r, s, MASKED)
        score[i % 2, c] = s
        top_run[i % 2] = jnp.maximum(top_run[i % 2], fold(s))

    def finish_top(i):
        best = jnp.max(top_run[i % 2], axis=1, keepdims=True)
        top[i % 2] = jnp.broadcast_to(best, (QB, PAGE))

    def mix(i, c):
        best = top[i % 2]
        s = score[i % 2, c]
        p = jnp.exp(s - jnp.concatenate([best] * (KC // PAGE), axis=1)).astype(BF16)
        acc[...] += jnp.dot(
            p, vals[pl.ds(pl.multiple_of(c * KC, KC), KC), :], preferred_element_type=F32
        )

    blocks = stretch // QB
    cached_chunks = span // KC

    top_run[0] = jnp.full((QB, PAGE), MASKED, F32)

    def first(c, _):
        make_scores(0, c, False)
        return 0

    lax.fori_loop(0, cached_chunks, first, 0)
    make_scores(0, cached_chunks, True)
    finish_top(0)
    for i in range(blocks):
        acc[...] = jnp.zeros_like(acc)
        chunks = cached_chunks + i + 1
        if i + 1 < blocks:
            top_run[(i + 1) % 2] = jnp.full((QB, PAGE), MASKED, F32)

            def both(c, _, i=i):
                make_scores(i + 1, c, False)
                mix(i, c)
                return 0

            lax.fori_loop(0, chunks, both, 0)
            make_scores(i + 1, chunks, True)
            finish_top(i + 1)
        else:

            def last(c, _, i=i):
                mix(i, c)
                return 0

            lax.fori_loop(0, chunks, last, 0)
        total = acc[...]
        result = pltpu.roll(total, HD, 1) / total
        out_ref[i * QB : (i + 1) * QB, :] = result[:, :HD].astype(BF16)

    slot_row = lax.broadcasted_iota(jnp.int32, (slots, PAGE), 0)
    slot_lane = lax.broadcasted_iota(jnp.int32, (slots, PAGE), 1)

    def fill_bias(i, _):
        seen = (slot_row == owner[i]) & (slot_lane < dcount[i])
        dbias[i] = jnp.where(seen, 0.0, MASKED)
        return 0

    lax.fori_loop(0, dnpages, fill_bias, 0)
    copy.wait()
    rows = mine_ref[...].astype(F32)
    heads = rows.shape[1] // (3 * HD)
    step = 1024
    per = step // PAGE
    for h in range(heads):
        block = h // 2 * PAGE
        width = heads * HD

        def part(which, left):
            piece = rows[:, which * width + block : which * width + block + PAGE]
            return pltpu.roll(piece, HD, 1) if (h % 2 == 1) == left else piece

        q = jnp.where(slot_lane < HD, part(0, True) * SCALE, 0.0)
        k = part(1, True)
        v = part(2, False)
        own = jnp.sum(q * k, axis=1, keepdims=True)
        qb = q.astype(BF16)
        best = jnp.broadcast_to(own, (slots, PAGE))
        for c in range(dspan // step):
            s = dot_nt(qb, dpool[c * step : (c + 1) * step, h * PAGE : (h + 1) * PAGE])
            s = s + jnp.concatenate([dbias[c * per + j] for j in range(per)], axis=1)
            dscore[c] = s
            best = jnp.maximum(best, fold(s))
        best = jnp.max(best, axis=1, keepdims=True)
        own_weight = jnp.exp(own - best)
        sums = jnp.zeros((slots, PAGE), F32)
        mixed = jnp.zeros((slots, PAGE), F32)
        for c in range(dspan // step):
            p = jnp.exp(dscore[c] - best)
            for j in range(per):
                sums = sums + p[:, j * PAGE : (j + 1) * PAGE]
            mixed = mixed + jnp.dot(
                p.astype(BF16),
                dpool[c * step : (c + 1) * step, h * PAGE : (h + 1) * PAGE],
                preferred_element_type=F32,
            )
        total = jnp.sum(sums, axis=1, keepdims=True) + own_weight
        mixed = (mixed + own_weight.astype(BF16).astype(F32) * v) / total
        dout_ref[:, h * HD : (h + 1) * HD] = pltpu.roll(mixed, HD, 1)[:, :HD].astype(BF16)


def attention(pages, length, dpages, dlens, qkv, mine, pool, dpool):
    stretch = qkv.shape[0]
    span = pool.shape[0]
    dspan, dwidth = dpool.shape
    slots = mine.shape[0]
    keys = span + stretch
    vmem = pl.BlockSpec(memory_space=pltpu.VMEM)
    smem = pl.BlockSpec(memory_space=pltpu.SMEM)
    return pl.pallas_call(
        attention_kernel,
        out_shape=(
            jax.ShapeDtypeStruct((stretch, HD), BF16),
            jax.ShapeDtypeStruct((slots, mine.shape[1] // 3), BF16),
        ),
        in_specs=[smem] * 4 + [vmem] * 3 + [pl.BlockSpec(memory_space=pl.ANY)],
        out_specs=(vmem, vmem),
        scratch_shapes=[
            pltpu.VMEM((keys, 2 * HD), BF16),
            pltpu.VMEM((keys, 2 * HD), BF16),
            pltpu.VMEM((stretch, 2 * HD), BF16),
            pltpu.VMEM((2, keys // KC, QB, KC), F32),
            pltpu.VMEM((2, QB, PAGE), F32),
            pltpu.VMEM((2, QB, PAGE), F32),
            pltpu.VMEM((QB, PAGE), F32),
            pltpu.VMEM((dspan, dwidth), BF16),
            pltpu.VMEM((dspan // PAGE, slots, PAGE), F32),
            pltpu.VMEM((dspan // 1024, slots, 1024), F32),
            pltpu.SMEM((span // PAGE,), jnp.int32),
            pltpu.SMEM((dspan // PAGE,), jnp.int32),
            pltpu.SMEM((dspan // PAGE,), jnp.int32),
            pltpu.SemaphoreType.DMA,
        ],
        compiler_params=pltpu.CompilerParams(vmem_limit_bytes=62 * 1024 * 1024),
        name="attention",
    )(pages, length, dpages, dlens, qkv, mine, pool, dpool)

MESH = pl.DeviceIdType.MESH
Q = 16


def ffn_kernel(
    block_ref,
    drow_ref,
    resid_ref,
    dresid_ref,
    wgu_hbm,
    wdown_hbm,
    out_ref,
    dout_ref,
    wgu,
    wdown,
    x,
    part,
    relay,
    direct,
    first,
    sums,
    relay1,
    direct1,
    xdec,
    xrows,
    pdec,
    rdec,
    wsem,
    ssem,
    rsem,
    dssem,
    drsem,
):
    me = lax.axis_index("tok")
    n_tok = lax.axis_size("tok")
    my_y, my_z = me // 4, me % 4
    barrier = pltpu.get_barrier_semaphore()
    for off in range(1, n_tok):
        pl.semaphore_signal(
            barrier,
            inc=1,
            device_id={"tok": (me + off) % n_tok},
            device_id_type=MESH,
        )
    load_gu = pltpu.make_async_copy(wgu_hbm, wgu, wsem.at[0])
    load_down = pltpu.make_async_copy(wdown_hbm, wdown, wsem.at[1])
    load_own = [
        pltpu.make_async_copy(
            block_ref.at[pl.ds(half * 2, 2)], x.at[half, 0, 0], wsem.at[2 + half]
        )
        for half in range(2)
    ]
    load_dec = pltpu.make_async_copy(drow_ref, xdec.at[0], wsem.at[4])
    for c in load_own:
        c.start()
    load_dec.start()
    load_gu.start()
    load_down.start()

    def along_z(step):
        return {"tok": my_y * 4 + (my_z + step + 4) % 4}

    def along_y(step):
        return {"tok": (my_y + step + 4) % 4 * 4 + my_z}

    axis1 = (along_z, along_y)
    axis2 = (along_y, along_z)
    used = [0]

    def send(source, target, device):
        i = used[0]
        used[0] += 1
        copy = pltpu.make_async_remote_copy(
            src_ref=source,
            dst_ref=target,
            send_sem=ssem.at[i],
            recv_sem=rsem.at[i],
            device_id=device,
            device_id_type=MESH,
        )
        copy.start()
        sent.append(copy)
        return copy

    sent = []
    for c in load_own:
        c.wait()
    load_dec.wait()
    pl.semaphore_wait(barrier, n_tok - 1)

    got = {}
    for half in range(2):
        own = x.at[half, 0, 0]
        got[half, 0, 3] = [send(own, x.at[half, 0, 3], axis1[half](1))]
        got[half, 0, 1] = [send(own, x.at[half, 0, 1], axis1[half](-1))]

    def spread(half, a1):
        own = x.at[half, 0, a1]
        got[half, 3, a1] = [send(own, x.at[half, 3, a1], axis2[half](1))]
        got[half, 1, a1] = [send(own, x.at[half, 1, a1], axis2[half](-1))]

    def relay2(half, a1):
        a = send(x.at[half, 3, a1, 0], x.at[half, 2, a1, 0], axis2[half](1))
        b = send(x.at[half, 1, a1, 1], x.at[half, 2, a1, 1], axis2[half](-1))
        got[half, 2, a1] = [a, b]

    def wait(half, a2, a1):
        for c in got[half, a2, a1]:
            c.wait_recv()

    for half in range(2):
        spread(half, 0)
    dec_copies = []
    for off in range(1, n_tok):
        copy = pltpu.make_async_remote_copy(
            src_ref=xdec.at[0],
            dst_ref=xdec.at[n_tok - off],
            send_sem=dssem.at[off],
            recv_sem=drsem.at[off],
            device_id={"tok": (me + off) % n_tok},
            device_id_type=MESH,
        )
        copy.start()
        dec_copies.append(copy)
    for half in range(2):
        wait(half, 0, 3)
        wait(half, 0, 1)
        a = send(x.at[half, 0, 3, 0], x.at[half, 0, 2, 0], axis1[half](1))
        b = send(x.at[half, 0, 1, 1], x.at[half, 0, 2, 1], axis1[half](-1))
        got[half, 0, 2] = [a, b]
        spread(half, 3)
        spread(half, 1)
    for half in range(2):
        wait(half, 3, 0)
        wait(half, 1, 0)
        relay2(half, 0)
    for half in range(2):
        wait(half, 0, 2)
        spread(half, 2)

    width = wdown.shape[0]

    def hidden_of(rows):
        both = dot_nt(rows, wgu[...])
        gate = both[:, :width]
        return (jax.nn.gelu(gate, approximate=True) * both[:, width:]).astype(BF16)

    def compute(half, a2):
        rows = x[half, a2].reshape(4 * 2 * Q, x.shape[-1])
        result = jnp.dot(hidden_of(rows), wdown[...], preferred_element_type=F32)
        part[half, a2] = result.astype(BF16).reshape(4, 2, Q, x.shape[-1])

    load_gu.wait()
    load_down.wait()

    def group0(i, _):
        compute(i, 0)
        return 0

    lax.fori_loop(0, 2, group0, 0)
    for a1 in (3, 1):
        for half in range(2):
            wait(half, 3, a1)
            wait(half, 1, a1)
            relay2(half, a1)
    for half in range(2):
        wait(half, 3, 2)
        wait(half, 1, 2)
        relay2(half, 2)

    def group13(i, _):
        compute(i % 2, 3 - 2 * (i // 2))
        return 0

    lax.fori_loop(0, 4, group13, 0)
    came = {}
    for half in range(2):
        came[half, 0, 1] = send(
            part.at[half, 1, :, 1], direct.at[half, 0, :, 1], axis2[half](1)
        )
        came[half, 1, 0] = send(
            part.at[half, 3, :, 0], direct.at[half, 1, :, 0], axis2[half](-1)
        )
    for c in dec_copies:
        c.wait_recv()
    for t in range(n_tok):
        xrows[t : t + 1, :] = xdec[t].astype(F32)
    dpart = jnp.dot(
        hidden_of(xrows[...].astype(BF16)), wdown[...], preferred_element_type=F32
    )
    for t in range(n_tok):
        pdec[t] = dpart[t : t + 1, :].astype(BF16)
    dec_back = []
    for off in range(1, n_tok):
        copy = pltpu.make_async_remote_copy(
            src_ref=pdec.at[off],
            dst_ref=rdec.at[n_tok - off],
            send_sem=dssem.at[n_tok + off],
            recv_sem=drsem.at[n_tok + off],
            device_id={"tok": (me + off) % n_tok},
            device_id_type=MESH,
        )
        copy.start()
        dec_back.append(copy)

    hop = {}
    for half in range(2):
        for a1 in range(4):
            wait(half, 2, a1)
        compute(half, 2)
        hop[half, 0] = send(part.at[half, 2, :, 0], relay.at[half, 0], axis2[half](1))
        hop[half, 1] = send(part.at[half, 2, :, 1], relay.at[half, 1], axis2[half](-1))
    for half in range(2):
        hop[half, 0].wait_recv()
        part[half, 1, :, 0] = (
            part[half, 1, :, 0].astype(F32) + relay[half, 0].astype(F32)
        ).astype(BF16)
        came[half, 0, 0] = send(
            part.at[half, 1, :, 0], direct.at[half, 0, :, 0], axis2[half](1)
        )
        hop[half, 1].wait_recv()
        part[half, 3, :, 1] = (
            part[half, 3, :, 1].astype(F32) + relay[half, 1].astype(F32)
        ).astype(BF16)
        came[half, 1, 1] = send(
            part.at[half, 3, :, 1], direct.at[half, 1, :, 1], axis2[half](-1)
        )
    dtotal = dresid_ref[...] + pdec[0].astype(F32)
    for c in dec_back:
        c.wait_recv()
    for off in range(1, n_tok):
        dtotal = dtotal + rdec[off].astype(F32)
    dout_ref[...] = dtotal.astype(BF16)
    hop1 = {}
    came1 = {}
    for half in range(2):
        for side in range(2):
            for q in range(2):
                came[half, side, q].wait_recv()
        for a1 in (2, 1, 3, 0):
            total = (
                part[half, 0, a1].astype(F32)
                + direct[half, 0, a1].astype(F32)
                + direct[half, 1, a1].astype(F32)
            )
            if a1 == 0:
                first[half] = total
            else:
                sums[half, a1] = total.astype(BF16)
            if a1 == 2:
                hop1[half, 0] = send(
                    sums.at[half, 2, 0], relay1.at[half, 0], axis1[half](1)
                )
                hop1[half, 1] = send(
                    sums.at[half, 2, 1], relay1.at[half, 1], axis1[half](-1)
                )
            if a1 == 1:
                came1[half, 0, 1] = send(
                    sums.at[half, 1, 1], direct1.at[half, 0, 1], axis1[half](1)
                )
            if a1 == 3:
                came1[half, 1, 0] = send(
                    sums.at[half, 3, 0], direct1.at[half, 1, 0], axis1[half](-1)
                )
    for half in range(2):
        hop1[half, 0].wait_recv()
        sums[half, 1, 0] = (
            sums[half, 1, 0].astype(F32) + relay1[half, 0].astype(F32)
        ).astype(BF16)
        came1[half, 0, 0] = send(
            sums.at[half, 1, 0], direct1.at[half, 0, 0], axis1[half](1)
        )
        hop1[half, 1].wait_recv()
        sums[half, 3, 1] = (
            sums[half, 3, 1].astype(F32) + relay1[half, 1].astype(F32)
        ).astype(BF16)
        came1[half, 1, 1] = send(
            sums.at[half, 3, 1], direct1.at[half, 1, 1], axis1[half](-1)
        )
    for half in range(2):
        for side in range(2):
            for q in range(2):
                came1[half, side, q].wait_recv()
        out_ref[half * 2 : half * 2 + 2] = (
            resid_ref[half * 2 : half * 2 + 2]
            + first[half]
            + direct1[half, 0].astype(F32)
            + direct1[half, 1].astype(F32)
        ).astype(BF16)
    for c in sent + dec_copies + dec_back:
        c.wait_send()


FFN_SENDS = 2 * (2 + 2 + 8 + 8 + 6 + 6)


def ffn(block, drow, resid, dresid, wgu, wdown, n_tok):
    width = block.shape[-1]
    vmem = pl.BlockSpec(memory_space=pltpu.VMEM)
    hbm = pl.BlockSpec(memory_space=pl.ANY)
    return pl.pallas_call(
        ffn_kernel,
        out_shape=(
            jax.ShapeDtypeStruct(block.shape, BF16),
            jax.ShapeDtypeStruct(drow.shape, BF16),
        ),
        in_specs=[vmem, vmem, vmem, vmem, hbm, hbm],
        out_specs=(vmem, vmem),
        scratch_shapes=[
            pltpu.VMEM(wgu.shape, BF16),
            pltpu.VMEM(wdown.shape, BF16),
            pltpu.VMEM((2, 4, 4, 2, Q, width), BF16),
            pltpu.VMEM((2, 4, 4, 2, Q, width), BF16),
            pltpu.VMEM((2, 2, 4, Q, width), BF16),
            pltpu.VMEM((2, 2, 4, 2, Q, width), BF16),
            pltpu.VMEM((2, 2, Q, width), F32),
            pltpu.VMEM((2, 4, 2, Q, width), BF16),
            pltpu.VMEM((2, 2, Q, width), BF16),
            pltpu.VMEM((2, 2, 2, Q, width), BF16),
            pltpu.VMEM((n_tok, 1, width), BF16),
            pltpu.VMEM((n_tok, width), F32),
            pltpu.VMEM((n_tok, 1, width), BF16),
            pltpu.VMEM((n_tok, 1, width), BF16),
            pltpu.SemaphoreType.DMA((5,)),
            pltpu.SemaphoreType.DMA((FFN_SENDS,)),
            pltpu.SemaphoreType.DMA((FFN_SENDS,)),
            pltpu.SemaphoreType.DMA((2 * n_tok,)),
            pltpu.SemaphoreType.DMA((2 * n_tok,)),
        ],
        compiler_params=pltpu.CompilerParams(
            collective_id=1, has_side_effects=True, vmem_limit_bytes=56 * 1024 * 1024
        ),
        name="ffn",
    )(block, drow, resid, dresid, wgu, wdown)


def shards(
    prefill_states,
    decode_states,
    attn_gain,
    w_qkv,
    w_out,
    ffn_gain,
    w_gate_up,
    w_down,
    prefill_pool,
    prefill_pages,
    prefill_lengths,
    prefill_home,
    decode_pool,
    decode_pages,
    decode_lengths,
    decode_home,
):
    n_tok = lax.axis_size("tok")
    n_head = lax.axis_size("head")
    my_tok = lax.axis_index("tok")
    my_head = lax.axis_index("head")
    requests, positions, width = prefill_states.shape
    hosted = decode_states.shape[0]
    heads_per = w_qkv.shape[2] // HD
    stretch = positions * n_tok
    units = requests * heads_per
    features = heads_per * HD
    normed_pre = rms_norm(prefill_states, attn_gain).reshape(requests * positions, width)
    normed_dec = rms_norm(decode_states, attn_gain)
    normed = jnp.concatenate([normed_pre, normed_dec], axis=0)
    projected = jnp.dot(
        normed, w_qkv.reshape(width, 3 * features), preferred_element_type=jnp.float32
    ).astype(jnp.bfloat16)
    proj_pre = projected[: requests * positions].reshape(requests, positions, 3, heads_per, HD)
    proj_dec = projected[requests * positions :]
    unit_ids = jnp.arange(units, dtype=jnp.int32)
    host_ids = jnp.arange(n_tok, dtype=jnp.int32)
    hosted_unit = jnp.sum(
        jnp.where(prefill_home[None, :] == host_ids[:, None], unit_ids[None, :], 0), axis=1
    )
    by_unit = jnp.transpose(proj_pre, (0, 3, 1, 2, 4)).reshape(units, positions * 3 * HD)
    outgoing = jnp.take(by_unit, hosted_unit, axis=0)
    pre_cols = positions * 3 * HD
    spread = jnp.broadcast_to(
        proj_dec.reshape(1, hosted * 3 * features), (n_tok, hosted * 3 * features)
    )
    outgoing = jnp.concatenate([outgoing, spread], axis=1)
    arrived = lax.all_to_all(outgoing, "tok", split_axis=0, concat_axis=0, tiled=True)
    arrived_dec = arrived[:, pre_cols:].reshape(n_tok * hosted, 3, heads_per, HD)
    arrived_pre = arrived[:, :pre_cols].reshape(stretch, 3, HD)
    my_unit = hosted_unit[my_tok]
    length = prefill_lengths[my_unit // heads_per]
    slots = my_tok * hosted + jnp.arange(hosted, dtype=jnp.int32)
    all_requests = jnp.arange(decode_home.shape[0], dtype=jnp.int32)
    anchor = jnp.sum(
        jnp.where(decode_home[None, :] == slots[:, None], all_requests[None, :], 0), axis=1
    )
    mine = jnp.take(arrived_dec, anchor, axis=0).reshape(hosted, 3 * features)
    qkv = jnp.pad(arrived_pre.reshape(stretch, 3 * HD), ((0, 0), (0, HD)))
    attn_unit, decode_attn = attention(
        prefill_pages,
        length.reshape(1),
        decode_pages,
        decode_lengths,
        qkv,
        mine,
        prefill_pool.reshape(-1, 2 * HD),
        decode_pool.reshape(-1, decode_pool.shape[2]),
    )
    backward = attn_unit.reshape(n_tok, positions * HD)
    back_cols = positions * HD
    spread_back = jnp.broadcast_to(
        decode_attn.reshape(1, hosted * features), (n_tok, hosted * features)
    )
    backward = jnp.concatenate([backward, spread_back], axis=1)
    returned = lax.all_to_all(backward, "tok", split_axis=0, concat_axis=0, tiled=True)
    by_slot = returned[:, back_cols:].reshape(n_tok * hosted, features)
    my_slots = lax.dynamic_slice_in_dim(decode_home, my_tok * hosted, hosted, 0)
    attn_dec = jnp.take(by_slot, my_slots, axis=0)
    attn_pre = jnp.take(returned[:, :back_cols], prefill_home, axis=0).reshape(
        requests, heads_per, positions, HD
    )
    block_rows = positions // n_head
    decode_share = hosted // n_head
    per = requests * block_rows + decode_share
    pre_rows = jnp.transpose(attn_pre, (0, 2, 1, 3)).reshape(requests, n_head, block_rows, features)
    pre_rows = jnp.transpose(pre_rows, (1, 0, 2, 3)).reshape(
        n_head, requests * block_rows, features
    )
    dec_rows = attn_dec.reshape(n_head, decode_share, features)
    ordered = jnp.concatenate([pre_rows, dec_rows], axis=1).reshape(n_head * per, features)
    mixed_rows = lax.psum_scatter(
        jnp.dot(ordered, w_out, preferred_element_type=jnp.float32).astype(jnp.bfloat16),
        "head",
        scatter_dimension=0,
        tiled=True,
    ).astype(jnp.float32)
    own_pre = lax.dynamic_slice_in_dim(prefill_states, my_head * block_rows, block_rows, 1).reshape(
        requests * block_rows, width
    )
    own_dec = lax.dynamic_slice_in_dim(decode_states, my_head * decode_share, decode_share, 0)
    resid = jnp.concatenate([own_pre, own_dec], axis=0).astype(jnp.float32) + mixed_rows
    normed_mid = rms_norm(resid, ffn_gain)
    rows = requests * block_rows
    prefill_out, decode_out = ffn(
        normed_mid[:rows].reshape(-1, Q, width),
        normed_mid[rows:],
        resid[:rows].reshape(-1, Q, width),
        resid[rows:],
        jnp.transpose(w_gate_up, (1, 2, 0)).reshape(-1, width),
        w_down,
        n_tok,
    )
    return (prefill_out, decode_out)


def solution(mesh):
    placed = (
        P(None, "tok", None),
        P("tok", None),
        P(),
        P(None, None, "head"),
        P("head", None),
        P(),
        P(None, None, "tok"),
        P("tok", None),
        P("tok", None, "head"),
        P("tok", None),
        P(),
        P(),
        P("tok", None, "head"),
        P("tok", None),
        P("tok"),
        P(),
    )
    return jax.shard_map(
        shards,
        mesh=mesh,
        in_specs=placed,
        out_specs=(P(None, ("tok", "head"), None), P(("tok", "head"), None)),
        check_vma=False,
    )
```

time: 710 us -> 222 us (0.31)
  other arithmetic: 200 us -> 6.98 us
  local copies, waits for them, and re-layouts: 193 us -> 42.8 us
  waiting for transfers between devices: 165 us -> 20.1 us
  Pallas kernels: 0 us -> 104 us
  matrix products: 76.3 us -> 3.52 us
  between operations: 17.5 us -> 4.38 us
  loops' own time: 8.49 us -> 0 us
    select_n x20 -> x2, other arithmetic: 141 us -> 0.68 us  [shards(): mine = jnp.take(arrived_dec, anchor, axis=0).reshape(hosted, 3 * features)]
    gather x18 -> x2, local copies, waits for them, and re-layouts: 106 us -> 0.68 us  [shards(): mine = jnp.take(arrived_dec, anchor, axis=0).reshape(hosted, 3 * features)]
    psum x1 -> x0, waiting for transfers between devices: 104 us -> none  [shards(): lax.psum(jnp.dot(hidden, w_down, preferred_element_type=jnp.float32).asty...]
    pallas_call x0 -> x2, Pallas kernels: none -> 104 us  [the longest x1 63 us: ffn(): pl.pallas_call(ffn_kernel, out_shape=(jax.ShapeDtypeStruct(block.shape, B...]
    dot_general x34 -> x0, matrix products: 70 us -> none  [the longest x4 17.3 us: attend(): jnp.dot(weight_cache.astype(jnp.bfloat16), cache_values, preferred_elemen...]
    all_gather x1 -> x0, waiting for transfers between devices: 53 us -> none  [shards(): piece = lax.all_gather(normed_mid, 'tok', axis=0, tiled=True)]
    slice x12 -> x4, local copies, waits for them, and re-layouts: 36.4 us -> 2.74 us  [the longest x1 0.83 us: shards(): resid[:rows].reshape(-1, Q, width)]
    reduce_sum x24 -> x0, other arithmetic: 21.8 us -> none  [the longest x4 13.9 us: attend(): jnp.sum(weight_cache, axis=1, keepdims=True)]
  transfers between devices with their start and end apart: 5 -> 3, of which waited for: 5 -> 3; matrix products, arithmetic and copies ran while one was open for 2% -> 1% of each run, Pallas kernels for 0% -> 0%
where the time goes in v1:
time: 222 us; the launch traced here: 218 us
  Pallas kernels  104 us (47%)
  local copies, waits for them, and re-layouts  42.8 us (19%)
  blocking collectives  23.9 us (11%)
  waiting for transfers between devices  20.1 us (9%)
  starting transfers between devices  13.3 us (6%)
  other arithmetic  6.98 us (3%)
  between operations  4.38 us (2%)
  matrix products  3.52 us (2%)
    pallas_call x1, Pallas kernels, ffn(): pl.pallas_call(ffn_kernel, out_shape=(jax.ShapeDtypeStruct(block.shape, B...  63 us
    pallas_call x1, Pallas kernels, attention(): pl.pallas_call(attention_kernel, out_shape=(jax.ShapeDtypeStruct((stretch...  40.5 us
    unnamed x1, blocking collectives  23.9 us
    unnamed x35, local copies, waits for them, and re-layouts  21.8 us
    all_to_all x1, waiting for transfers between devices, shards(): lax.all_to_all(outgoing, 'tok', split_axis=0, concat_axis=0, tiled=True)  11.4 us
    all_to_all x1, starting transfers between devices, shards(): lax.all_to_all(outgoing, 'tok', split_axis=0, concat_axis=0, tiled=True)  8.21 us
    all_to_all x1, waiting for transfers between devices, shards(): lax.all_to_all(backward, 'tok', split_axis=0, concat_axis=0, tiled=True)  7.77 us
  transfers between devices with their start and end apart: 3, of which 3 were waited for; matrix products, arithmetic and copies ran while one was open for 1% of the time, Pallas kernels for 0%

profile of v1, /device:TPU:0, one launch (start us, length us, event | category | flops | bytes accessed | tf_op | source)
XLA Modules:
  0.0 218.5 jit_solution(3605094578261592156)
XLA Ops:
  2.2 4.9 %copy.42 = bf16[2048,3,256]{0,2,1:T(8,128)(2,1)} copy(bf16[2048,3,256]{2,0,1:T(8,128)(2,1)} %param.19) | data formatting | bytes 6291456 | tf_op args[3]
  8.4 1.3 copy-done.2
  9.6 1.8 fusion.8
  12.4 2.6 %copy.44 = bf16[4,4,128,3,64]{4,3,2,1,0:T(4,128)(2,1)} copy(bf16[4,4,128,3,64]{2,0,4,1,3:T(4,128)(2,1)S(1)} %bitcast.50) | data formatting | bytes 1572864 | tf_op jit(solution)/shard_map/transpose | solution.py:649
  15.0 2.9 %reshape.177 = bf16[16,24576]{1,0:T(8,128)(2,1)S(1)} reshape(bf16[4,4,128,3,64]{4,3,2,1,0:T(4,128)(2,1)} %copy.44) | data formatting | bytes 1572864 | tf_op jit(solution)/shard_map/reshape | solution.py:649
  17.9 1.1 gather_fusion
  19.9 1.4 reduce
  21.3 1.7 reshape.226
  23.0 8.2 %all-to-all-start = ((bf16[16,2,15360]{2,1,0:T(2,128)(2,1)}), bf16[16,2,15360]{2,1,0:T(2,128)(2,1)}, u32[]{:S(2)}, u32[]{:S(2)}) async-start(bf16[16,2,15360]{2,1,0:T(2,128)(2,1)} %reshape.226), calls=%async_computation | async-start | bytes 1966080 | tf_op jit(solution)/shard_map/all_to_all | solution.py:656
  36.8 11.4 %all-to-all-done = bf16[16,2,15360]{2,1,0:T(2,128)(2,1)} async-done(((bf16[16,2,15360]{2,1,0:T(2,128)(2,1)}), bf16[16,2,15360]{2,1,0:T(2,128)(2,1)}, u32[]{:S(2)}, u32[]{:S(2)}) %all-to-all-start) | async-done | bytes 983072 | tf_op jit(solution)/shard_map/all_to_all | solution.py:656
  48.2 4.1 %reshape.227 = bf16[16,1,30720]{2,1,0:T(2,128)(2,1)S(1)} reshape(bf16[16,2,15360]{2,1,0:T(2,128)(2,1)} %all-to-all-done) | data formatting | bytes 1966080
  53.0 1.2 reshape_reshape.3
  55.3 1.2 pad.4.qkv_ref
  57.1 40.5 %attention.1 = (bf16[2048,64]{1,0:T(8,128)(2,1)}, bf16[8,256]{1,0:T(8,128)(2,1)}) custom-call(s32[1,48]{1,0:T(1,128)} %pages.1, s32[1]{0:T(128)} %dynamic_slice.18.length_ref, s32[8,32]{1,0:T(8,128)} %dpages.1, s32[8]{0:T(128)} %dlens.1, bf16[2048,256]{1,0:T(8,128)(2,1)} %pad.4.qkv_ref, bf16[8,768]{1,0:T(8,128)(2,1)} %broadcast_select_fusion.1.mine_ref, ...), custom_call_target="tpu_custom_call" | custom-call | tf_op jit(solution)/shard_map/attention/pallas_call | solution.py:244
  97.7 1.5 reshape.181
  101.7 3.5 %all-to-all-start.1 = ((bf16[16,2,5120]{2,1,0:T(2,128)(2,1)}), bf16[16,2,5120]{2,1,0:T(2,128)(2,1)S(1)}, u32[]{:S(2)}, u32[]{:S(2)}) async-start(bf16[16,2,5120]{2,1,0:T(2,128)(2,1)} %reshape.228), calls=%async_computation.1 | async-start | bytes 655360 | tf_op jit(solution)/shard_map/all_to_all | solution.py:684
  106.3 7.8 %all-to-all-done.1 = bf16[16,2,5120]{2,1,0:T(2,128)(2,1)S(1)} async-done(((bf16[16,2,5120]{2,1,0:T(2,128)(2,1)}), bf16[16,2,5120]{2,1,0:T(2,128)(2,1)S(1)}, u32[]{:S(2)}, u32[]{:S(2)}) %all-to-all-start.1) | async-done | bytes 327712 | tf_op jit(solution)/shard_map/all_to_all | solution.py:684
  118.3 1.7 convolution_convert_fusion
  120.0 23.9 %fusion = bf16[72,2048]{1,0:T(8,128)(2,1)} fusion(bf16[520,2048]{1,0:T(8,128)(2,1)S(1)} %convolution_convert_fusion), kind=kCustom, calls=%all-reduce-scatter | all-reduce-scatter fusion | flops 1179649 | bytes 2425344
  144.9 1.5 collective-permute-start
  147.2 2.1 concatenate.20
  152.5 63.0 %ffn.1 = (bf16[4,16,2048]{2,1,0:T(8,128)(2,1)}, bf16[1,2048]{1,0:T(2,128)(2,1)}) custom-call(bf16[4,16,2048]{2,1,0:T(8,128)(2,1)} %bitcast.59, bf16[1,2048]{1,0:T(2,128)(2,1)} %slice.55.drow_ref, f32[4,16,2048]{2,1,0:T(8,128)} %bitcast.54, f32[1,2048]{1,0:T(1,128)} %slice.57.dresid_ref, bf16[640,2048]{1,0:T(8,128)(2,1)} %bitcast.51, bf16[320,2048]{1,0:T(8,128)(2,1)} %wdown_hbm.1), custom_call_target="tpu_custom_call" | custom-call | tf_op jit(solution)/shard_map/ffn/pallas_call | solution.py:572
  215.5 1.7 copy.61
  217.2 1.3 copy.62
  (92 shorter events, 21.9 us)
Async XLA Ops:
  0.6 117.6 %copy-start = (bf16[256,2048]{1,0:T(8,128)(2,1)S(1)}, bf16[256,2048]{1,0:T(8,128)(2,1)}, u32[]{:S(2)}) copy-start(bf16[256,2048]{1,0:T(8,128)(2,1)} %param.20) | copy-start | bytes 3145732
  2.2 4.9 %copy-start.4 = (bf16[8,2048]{1,0:T(8,128)(2,1)S(1)}, bf16[8,2048]{1,0:T(8,128)(2,1)}, u32[]{:S(2)}) copy-start(bf16[8,2048]{1,0:T(8,128)(2,1)} %param.17) | copy-start | bytes 98308
  2.2 5.0 %copy-start.1 = (bf16[4,128,2048]{2,1,0:T(8,128)(2,1)S(1)}, bf16[4,128,2048]{2,1,0:T(8,128)(2,1)}, u32[]{:S(2)}) copy-start(bf16[4,128,2048]{2,1,0:T(8,128)(2,1)} %param.16) | copy-start | bytes 6291460
  7.1 0.7 copy-start.5
  7.8 1.9 copy-start.2
  11.5 0.9 copy-start.3
  15.0 2.9 %slice-start = ((bf16[520,768]{1,0:T(8,128)(2,1)}), bf16[8,768]{1,0:T(8,128)(2,1)S(1)}, s32[]{:S(2)}) async-start(bf16[520,768]{1,0:T(8,128)(2,1)} %copy-done.3), calls=%async_computation.2 | async-start | bytes 24576 | tf_op jit(solution)/shard_map/slice | solution.py:643
  21.3 10.0 %copy-start.8 = (s32[128]{0:T(128)S(1)}, s32[128]{0:T(128)}, u32[]{:S(2)}) copy-start(s32[128]{0:T(128)} %param.31) | copy-start | bytes 1540
  21.3 13.5 %copy-start.10 = (s32[4]{0:T(128)S(1)}, s32[4]{0:T(128)}, u32[]{:S(2)}) copy-start(s32[4]{0:T(128)} %param.26) | copy-start | bytes 52
  21.3 14.1 %copy-start.7 = (u32[128]{0:T(128)S(1)}, u32[128]{0:T(128)}, u32[]{:S(2)}) copy-start(u32[128]{0:T(128)} %constant.107) | copy-start | bytes 1540
  21.3 15.5 %copy-start.9 = (s32[16]{0:T(128)S(1)}, s32[16]{0:T(128)}, u32[]{:S(2)}) copy-start(s32[16]{0:T(128)} %param.27) | copy-start | bytes 196
  23.0 25.2 %all-to-all-start = ((bf16[16,2,15360]{2,1,0:T(2,128)(2,1)}), bf16[16,2,15360]{2,1,0:T(2,128)(2,1)}, u32[]{:S(2)}, u32[]{:S(2)}) async-start(bf16[16,2,15360]{2,1,0:T(2,128)(2,1)} %reshape.226), calls=%async_computation | async-start | bytes 1966080 | tf_op jit(solution)/shard_map/all_to_all | solution.py:656
  101.7 12.3 %all-to-all-start.1 = ((bf16[16,2,5120]{2,1,0:T(2,128)(2,1)}), bf16[16,2,5120]{2,1,0:T(2,128)(2,1)S(1)}, u32[]{:S(2)}, u32[]{:S(2)}) async-start(bf16[16,2,5120]{2,1,0:T(2,128)(2,1)} %reshape.228), calls=%async_computation.1 | async-start | bytes 655360 | tf_op jit(solution)/shard_map/all_to_all | solution.py:684
  119.9 29.6 %copy-start.6 = (f32[2048]{0:T(1024)S(1)}, f32[2048]{0:T(1024)}, u32[]{:S(2)}) copy-start(f32[2048]{0:T(1024)} %param.21) | copy-start | bytes 24580
  144.9 2.4 %collective-permute-start = (bf16[49,2048]{1,0:T(8,128)(2,1)S(1)}, bf16[49,2048]{1,0:T(8,128)(2,1)S(1)}, u32[]{:S(2)}, u32[]{:S(2)}) collective-permute-start(bf16[49,2048]{1,0:T(8,128)(2,1)S(1)} %slice.58), channel_id=1, source_target_pairs={{0,1},{1,2},{2,3},{3,4},{4,5},{5,6},{6,7},{8,9},{9,10},{10,11},{11... | collective-permute-start | bytes 602120

commit v2 on v1

--- a/solution.py
+++ b/solution.py
@@ -1,5 +1,3 @@
-import math
-
 import jax
 import jax.numpy as jnp
 from jax import lax
@@ -32,11 +30,13 @@
 
 def attention_kernel(
     pages,
-    length_ref,
+    lengths,
+    homes,
     dpages,
     dlens,
-    qkv_ref,
-    mine_ref,
+    dhomes,
+    arrived,
+    arrived_dec,
     pool_ref,
     dpool_hbm,
     out_ref,
@@ -51,12 +51,18 @@
     dpool,
     dbias,
     dscore,
+    drows,
+    mine_ref,
     count,
     owner,
     dcount,
+    anchor,
     sem,
 ):
-    stretch = qkv_ref.shape[0]
+    me = lax.axis_index("tok")
+    n_tok = arrived.shape[0]
+    positions = arrived.shape[1] // 3 * 2
+    stretch = n_tok * positions
     span = pool_ref.shape[0]
     npages = span // PAGE
     dspan = dpool_hbm.shape[0]
@@ -65,7 +71,10 @@
     copy = pltpu.make_async_copy(dpool_hbm, dpool, sem)
     copy.start()
 
-    length = length_ref[0]
+    my_unit = jnp.int32(0)
+    for u in range(n_tok):
+        my_unit = jnp.where(homes[u] == me, u, my_unit)
+    length = lengths[my_unit // (n_tok // lengths.shape[0])]
 
     def count_page(i, _):
         count[pages[0, i]] = jnp.clip(length - i * PAGE, 0, PAGE)
@@ -103,16 +112,21 @@
 
     lax.fori_loop(0, npages, fill_cached, 0)
 
+    half = PAGE // 2
+
     def fill_own(i, _):
-        source = pl.ds(pl.multiple_of(i * PAGE, PAGE), PAGE)
         target = pl.ds(pl.multiple_of(span + i * PAGE, PAGE), PAGE)
-        left = qkv_ref[source, :PAGE].astype(F32)
-        right = qkv_ref[source, PAGE:].astype(F32)
-        query[source, :] = jnp.where(
-            lane < HD, left * SCALE, jnp.where(lane == HD, 1.0, 0.0)
-        ).astype(BF16)
-        keys[target, :] = jnp.where(lane < HD, pltpu.roll(left, HD, 1), 0.0).astype(BF16)
-        vals[target, :] = jnp.where(lane < HD, 1.0, pltpu.roll(right, HD, 1)).astype(BF16)
+        both = arrived[i, :PAGE, :].astype(F32)
+        keys[target, :] = jnp.where(lane < HD, both, 0.0).astype(BF16)
+        vals[target, :] = jnp.where(lane < HD, 1.0, both).astype(BF16)
+        packed = arrived[i, PAGE:, :].astype(F32) * SCALE
+        flag = jnp.where(lane[:half] == HD, 1.0, 0.0)
+        low = jnp.where(lane[:half] < HD, packed, flag)
+        high = jnp.where(lane[:half] < HD, pltpu.roll(packed, HD, 1), flag)
+        at_low = pl.ds(pl.multiple_of(i * PAGE, PAGE), half)
+        at_high = pl.ds(pl.multiple_of(i * PAGE + half, half), half)
+        query[at_low, :] = low.astype(BF16)
+        query[at_high, :] = high.astype(BF16)
         return 0
 
     lax.fori_loop(0, stretch // PAGE, fill_own, 0)
@@ -180,7 +194,11 @@
             lax.fori_loop(0, chunks, last, 0)
         total = acc[...]
         result = pltpu.roll(total, HD, 1) / total
-        out_ref[i * QB : (i + 1) * QB, :] = result[:, :HD].astype(BF16)
+        for j in range(QB // PAGE):
+            tile = result[j * PAGE : (j + 1) * PAGE]
+            out_ref[i * (QB // PAGE) + j] = jnp.where(
+                lane[:half] < HD, tile[:half], pltpu.roll(tile[half:], HD, 1)
+            ).astype(BF16)
 
     slot_row = lax.broadcasted_iota(jnp.int32, (slots, PAGE), 0)
     slot_lane = lax.broadcasted_iota(jnp.int32, (slots, PAGE), 1)
@@ -191,8 +209,23 @@
         return 0
 
     lax.fori_loop(0, dnpages, fill_bias, 0)
+    for t in range(n_tok):
+        drows[t * slots : (t + 1) * slots, :] = arrived_dec[t].astype(F32)
+
+    def find(r, _):
+        slot = dhomes[r] - me * slots
+
+        @pl.when((slot >= 0) & (slot < slots))
+        def _():
+            anchor[slot] = r
+
+        return 0
+
+    lax.fori_loop(0, dhomes.shape[0], find, 0)
+    for s in range(slots):
+        mine_ref[s : s + 1, :] = drows[pl.ds(anchor[s], 1), :]
     copy.wait()
-    rows = mine_ref[...].astype(F32)
+    rows = mine_ref[...]
     heads = rows.shape[1] // (3 * HD)
     step = 1024
     per = step // PAGE
@@ -233,21 +266,25 @@
         dout_ref[:, h * HD : (h + 1) * HD] = pltpu.roll(mixed, HD, 1)[:, :HD].astype(BF16)
 
 
-def attention(pages, length, dpages, dlens, qkv, mine, pool, dpool):
-    stretch = qkv.shape[0]
+def attention(
+    pages, lengths, homes, dpages, dlens, dhomes, arrived, arrived_dec, pool, dpool
+):
+    n_tok, packed, lanes = arrived.shape
+    positions = packed // 3 * 2
+    stretch = n_tok * positions
     span = pool.shape[0]
     dspan, dwidth = dpool.shape
-    slots = mine.shape[0]
+    slots, dcols = arrived_dec.shape[1:]
     keys = span + stretch
     vmem = pl.BlockSpec(memory_space=pltpu.VMEM)
     smem = pl.BlockSpec(memory_space=pltpu.SMEM)
     return pl.pallas_call(
         attention_kernel,
         out_shape=(
-            jax.ShapeDtypeStruct((stretch, HD), BF16),
-            jax.ShapeDtypeStruct((slots, mine.shape[1] // 3), BF16),
+            jax.ShapeDtypeStruct((n_tok, positions // 2, lanes), BF16),
+            jax.ShapeDtypeStruct((slots, dcols // 3), BF16),
         ),
-        in_specs=[smem] * 4 + [vmem] * 3 + [pl.BlockSpec(memory_space=pl.ANY)],
+        in_specs=[smem] * 6 + [vmem] * 3 + [pl.BlockSpec(memory_space=pl.ANY)],
         out_specs=(vmem, vmem),
         scratch_shapes=[
             pltpu.VMEM((keys, 2 * HD), BF16),
@@ -260,14 +297,18 @@
             pltpu.VMEM((dspan, dwidth), BF16),
             pltpu.VMEM((dspan // PAGE, slots, PAGE), F32),
             pltpu.VMEM((dspan // 1024, slots, 1024), F32),
+            pltpu.VMEM((n_tok * slots, dcols), F32),
+            pltpu.VMEM((slots, dcols), F32),
             pltpu.SMEM((span // PAGE,), jnp.int32),
             pltpu.SMEM((dspan // PAGE,), jnp.int32),
             pltpu.SMEM((dspan // PAGE,), jnp.int32),
+            pltpu.SMEM((slots,), jnp.int32),
             pltpu.SemaphoreType.DMA,
         ],
         compiler_params=pltpu.CompilerParams(vmem_limit_bytes=62 * 1024 * 1024),
         name="attention",
-    )(pages, length, dpages, dlens, qkv, mine, pool, dpool)
+    )(pages, lengths, homes, dpages, dlens, dhomes, arrived, arrived_dec, pool, dpool)
+
 
 MESH = pl.DeviceIdType.MESH
 Q = 16
@@ -605,6 +646,401 @@
     )(block, drow, resid, dresid, wgu, wdown)
 
 
+def project_kernel(
+    states,
+    dstates,
+    gain_ref,
+    w_hbm,
+    homes,
+    out_ref,
+    dec_ref,
+    w,
+    normed,
+    units,
+    outgoing,
+    pdec,
+    wsem,
+    lsem,
+    ssem,
+    rsem,
+    dssem,
+    drsem,
+):
+    me = lax.axis_index("tok")
+    n_tok = lax.axis_size("tok")
+    requests, positions, width = states.shape
+    features = w.shape[2]
+    per = features // HD
+    barrier = pltpu.get_barrier_semaphore()
+    for off in range(1, n_tok):
+        pl.semaphore_signal(
+            barrier, inc=1, device_id={"tok": (me + off) % n_tok}, device_id_type=MESH
+        )
+    load = pltpu.make_async_copy(w_hbm, w, wsem)
+    load.start()
+    gain = gain_ref[...]
+    pdec_rows = rms_norm(dstates[...], gain)
+    lane = lax.broadcasted_iota(jnp.int32, (positions, PAGE), 1)
+    half = positions // 2
+
+    strip = 64
+
+    def norm(i, _):
+        at = pl.ds(pl.multiple_of(i % (positions // strip) * strip, strip), strip)
+        normed[i] = rms_norm(states[i // (positions // strip), at, :], gain)
+        return 0
+
+    lax.fori_loop(0, requests * positions // strip, norm, 0)
+    load.wait()
+    pl.semaphore_wait(barrier, n_tok - 1)
+    for which in range(3):
+        pdec[:, which * features : (which + 1) * features] = jnp.dot(
+            pdec_rows, w[which], preferred_element_type=F32
+        ).astype(BF16)
+    copies = []
+    for off in range(1, n_tok):
+        copy = pltpu.make_async_remote_copy(
+            src_ref=pdec,
+            dst_ref=dec_ref.at[me],
+            send_sem=dssem.at[off],
+            recv_sem=drsem.at[off],
+            device_id={"tok": (me + off) % n_tok},
+            device_id_type=MESH,
+        )
+        copy.start()
+        copies.append(copy)
+
+    def project(r, _):
+        rows = normed[pl.ds(r * (positions // strip), positions // strip)].reshape(
+            positions, width
+        )
+        q, k, v = (jnp.dot(rows, w[i], preferred_element_type=F32) for i in range(3))
+        for j in range(per):
+            at = j // 2 * PAGE
+            qb, kb, vb = (a[:, at : at + PAGE] for a in (q, k, v))
+            if j % 2 == 0:
+                both = jnp.where(lane < HD, kb, pltpu.roll(vb, HD, 1))
+                pair = jnp.where(lane[:half] < HD, qb[:half], pltpu.roll(qb[half:], HD, 1))
+            else:
+                both = jnp.where(lane < HD, pltpu.roll(kb, HD, 1), vb)
+                pair = jnp.where(lane[:half] < HD, pltpu.roll(qb[:half], HD, 1), qb[half:])
+            units[r * per + j, :positions, :] = both.astype(BF16)
+            units[r * per + j, positions:, :] = pair.astype(BF16)
+        return 0
+
+    lax.fori_loop(0, requests, project, 0)
+    for off in range(n_tok):
+        target = (me + off) % n_tok
+        unit = jnp.int32(0)
+        for u in range(requests * per):
+            unit = jnp.where(homes[u] == target, u, unit)
+        if off == 0:
+            outgoing[0] = units[unit]
+            own = pltpu.make_async_copy(outgoing.at[0], out_ref.at[me], lsem.at[0])
+            own_dec = pltpu.make_async_copy(pdec, dec_ref.at[me], lsem.at[1])
+            own.start()
+            own_dec.start()
+            continue
+        outgoing[off] = units[unit]
+        copy = pltpu.make_async_remote_copy(
+            src_ref=outgoing.at[off],
+            dst_ref=out_ref.at[me],
+            send_sem=ssem.at[off],
+            recv_sem=rsem.at[off],
+            device_id={"tok": target},
+            device_id_type=MESH,
+        )
+        copy.start()
+        copies.append(copy)
+    own.wait()
+    own_dec.wait()
+    for copy in copies:
+        copy.wait()
+
+
+def project(states, dstates, gain, w, homes, n_tok):
+    requests, positions, width = states.shape
+    hosted = dstates.shape[0]
+    features = w.shape[2]
+    vmem = pl.BlockSpec(memory_space=pltpu.VMEM)
+    smem = pl.BlockSpec(memory_space=pltpu.SMEM)
+    packed = positions // 2 * 3
+    units = requests * features // HD
+    return pl.pallas_call(
+        project_kernel,
+        out_shape=(
+            jax.ShapeDtypeStruct((n_tok, packed, 2 * HD), BF16),
+            jax.ShapeDtypeStruct((n_tok, hosted, 3 * features), BF16),
+        ),
+        in_specs=[vmem, vmem, vmem, pl.BlockSpec(memory_space=pl.ANY), smem],
+        out_specs=(vmem, vmem),
+        scratch_shapes=[
+            pltpu.VMEM(w.shape, BF16),
+            pltpu.VMEM((requests * positions // 64, 64, width), BF16),
+            pltpu.VMEM((units, packed, 2 * HD), BF16),
+            pltpu.VMEM((n_tok, packed, 2 * HD), BF16),
+            pltpu.VMEM((hosted, 3 * features), BF16),
+            pltpu.SemaphoreType.DMA,
+            pltpu.SemaphoreType.DMA((2,)),
+            pltpu.SemaphoreType.DMA((n_tok,)),
+            pltpu.SemaphoreType.DMA((n_tok,)),
+            pltpu.SemaphoreType.DMA((n_tok,)),
+            pltpu.SemaphoreType.DMA((n_tok,)),
+        ],
+        compiler_params=pltpu.CompilerParams(
+            collective_id=2, has_side_effects=True, vmem_limit_bytes=56 * 1024 * 1024
+        ),
+        name="project",
+    )(states, dstates, gain, w, homes)
+
+
+def mix_kernel(
+    attn,
+    dattn,
+    states_hbm,
+    dstates,
+    gain_ref,
+    w_hbm,
+    homes,
+    dhomes,
+    normed_ref,
+    dnormed_ref,
+    resid_ref,
+    dresid_ref,
+    w,
+    own,
+    drows,
+    got,
+    gdec,
+    gdec_rows,
+    left,
+    dleft,
+    part,
+    pdec,
+    rdec,
+    pair,
+    sums,
+    relay,
+    direct,
+    lsem,
+    tssem,
+    trsem,
+    dssem,
+    drsem,
+    hssem,
+    hrsem,
+    ssem,
+    rsem,
+):
+    me = lax.axis_index("tok")
+    n_tok = lax.axis_size("tok")
+    head = lax.axis_index("head")
+    n_head = lax.axis_size("head")
+    my_x, core = head // 2, head % 2
+    n_x = n_head // 2
+    requests, rows, width = own.shape
+    positions = rows * n_head
+    half = positions // 2
+    hosted = dattn.shape[0]
+    barrier = pltpu.get_barrier_semaphore()
+    for off in range(1, n_tok):
+        pl.semaphore_signal(
+            barrier, inc=1, device_id={"tok": (me + off) % n_tok}, device_id_type=MESH
+        )
+    for off in range(1, n_head):
+        pl.semaphore_signal(
+            barrier, inc=1, device_id={"head": (head + off) % n_head}, device_id_type=MESH
+        )
+    load_w = pltpu.make_async_copy(w_hbm, w, lsem.at[0])
+    load_own = pltpu.make_async_copy(
+        states_hbm.at[:, pl.ds(pl.multiple_of(head * rows, rows), rows), :], own, lsem.at[1]
+    )
+    keep = pltpu.make_async_copy(attn.at[me], got.at[me], lsem.at[2])
+    keep_dec = pltpu.make_async_copy(dattn, gdec.at[me], lsem.at[3])
+    local = [load_w, load_own, keep, keep_dec]
+    for c in local:
+        c.start()
+    pl.semaphore_wait(barrier, n_tok + n_head - 2)
+    sends = []
+    for off in range(1, n_tok):
+        target = (me + off) % n_tok
+        for source, dest, a, b in (
+            (attn.at[target], got.at[me], tssem, trsem),
+            (dattn, gdec.at[me], dssem, drsem),
+        ):
+            copy = pltpu.make_async_remote_copy(
+                src_ref=source,
+                dst_ref=dest,
+                send_sem=a.at[off],
+                recv_sem=b.at[off],
+                device_id={"tok": target},
+                device_id_type=MESH,
+            )
+            copy.start()
+            sends.append(copy)
+    drows[...] = dstates[...].astype(F32)
+    for c in local:
+        c.wait()
+    for c in sends:
+        c.wait_recv()
+    lane = lax.broadcasted_iota(jnp.int32, (half, PAGE), 1)
+    per = w.shape[0] // HD
+    for r in range(requests):
+        for j in range(0, per, 2):
+            a = got[homes[r * per + j]].astype(F32)
+            b = got[homes[r * per + j + 1]].astype(F32)
+            low = jnp.where(lane < HD, a, pltpu.roll(b, HD, 1))
+            high = jnp.where(lane < HD, pltpu.roll(a, HD, 1), b)
+            cols = slice(j // 2 * PAGE, (j // 2 + 1) * PAGE)
+            left[r, :half, cols] = low.astype(BF16)
+            left[r, half:, cols] = high.astype(BF16)
+    for t in range(n_tok):
+        gdec_rows[t * hosted : (t + 1) * hosted, :] = gdec[t].astype(F32)
+    for i in range(hosted):
+        dleft[i : i + 1, :] = gdec_rows[pl.ds(dhomes[me * hosted + i], 1), :]
+
+    def project(r, _):
+        result = jnp.dot(left[r], w[...], preferred_element_type=F32).astype(BF16)
+        for k in range(n_head):
+            part[k % 2, r, k // 2] = result[k * rows : (k + 1) * rows]
+        return 0
+
+    lax.fori_loop(0, requests, project, 0)
+    used = [0]
+    ring = []
+
+    def send(source, target, device):
+        i = used[0]
+        used[0] += 1
+        copy = pltpu.make_async_remote_copy(
+            src_ref=source,
+            dst_ref=target,
+            send_sem=ssem.at[i],
+            recv_sem=rsem.at[i],
+            device_id={"head": device},
+            device_id_type=MESH,
+        )
+        copy.start()
+        ring.append(copy)
+        return copy
+
+    partner = my_x * 2 + 1 - core
+    up = (my_x + 1) % n_x * 2 + core
+    down = (my_x + n_x - 1) % n_x * 2 + core
+    order = (2, 1, 3, 0)
+    paired = {}
+    for dx in order:
+        paired[dx] = send(
+            part.at[1 - core, :, (my_x + dx) % n_x], pair.at[dx], partner
+        )
+    dresult = jnp.dot(dleft[...].astype(BF16), w[...], preferred_element_type=F32)
+    for k in range(n_head):
+        pdec[k] = dresult[k : k + 1, :].astype(BF16)
+    for off in range(1, n_head):
+        copy = pltpu.make_async_remote_copy(
+            src_ref=pdec.at[(head + off) % n_head],
+            dst_ref=rdec.at[n_head - off],
+            send_sem=hssem.at[off],
+            recv_sem=hrsem.at[off],
+            device_id={"head": (head + off) % n_head},
+            device_id_type=MESH,
+        )
+        copy.start()
+        sends.append(copy)
+    hop = {}
+    came = {}
+    for dx in order:
+        paired[dx].wait_recv()
+        total = part[core, :, (my_x + dx) % n_x].astype(F32) + pair[dx].astype(F32)
+        if dx == 0:
+            resid_ref[...] = total + own[...].astype(F32)
+        else:
+            sums[dx] = total.astype(BF16)
+        if dx == 2:
+            hop[0] = send(sums.at[2, 0:2], relay.at[0], up)
+            hop[1] = send(sums.at[2, 2:4], relay.at[1], down)
+        if dx == 1:
+            came[0, 1] = send(sums.at[1, 2:4], direct.at[0, 2:4], up)
+        if dx == 3:
+            came[1, 0] = send(sums.at[3, 0:2], direct.at[1, 0:2], down)
+    hop[0].wait_recv()
+    sums[1, 0:2] = (sums[1, 0:2].astype(F32) + relay[0].astype(F32)).astype(BF16)
+    came[0, 0] = send(sums.at[1, 0:2], direct.at[0, 0:2], up)
+    hop[1].wait_recv()
+    sums[3, 2:4] = (sums[3, 2:4].astype(F32) + relay[1].astype(F32)).astype(BF16)
+    came[1, 1] = send(sums.at[3, 2:4], direct.at[1, 2:4], down)
+    gain = gain_ref[...]
+    dtotal = drows[pl.ds(head, 1), :] + pdec[head].astype(F32)
+    for c in sends[2 * (n_tok - 1) :]:
+        c.wait_recv()
+    for off in range(1, n_head):
+        dtotal = dtotal + rdec[off].astype(F32)
+    dresid_ref[...] = dtotal
+    dnormed_ref[...] = rms_norm(dtotal, gain)
+    for c in came.values():
+        c.wait_recv()
+    for r in range(requests):
+        total = resid_ref[r] + direct[0, r].astype(F32) + direct[1, r].astype(F32)
+        resid_ref[r] = total
+        normed_ref[r] = rms_norm(total, gain)
+    for c in sends + ring:
+        c.wait_send()
+
+
+def mix(attn, dattn, states, dstates, gain, w, homes, dhomes, n_head):
+    requests, positions, width = states.shape
+    n_tok, packed, lanes = attn.shape
+    hosted = dattn.shape[0]
+    rows = positions // n_head
+    n_x = n_head // 2
+    vmem = pl.BlockSpec(memory_space=pltpu.VMEM)
+    smem = pl.BlockSpec(memory_space=pltpu.SMEM)
+    hbm = pl.BlockSpec(memory_space=pl.ANY)
+    sem = pltpu.SemaphoreType.DMA
+    ring = 4 + 6
+    return pl.pallas_call(
+        mix_kernel,
+        out_shape=(
+            jax.ShapeDtypeStruct((requests, rows, width), BF16),
+            jax.ShapeDtypeStruct((1, width), BF16),
+            jax.ShapeDtypeStruct((requests, rows, width), F32),
+            jax.ShapeDtypeStruct((1, width), F32),
+        ),
+        in_specs=[vmem, vmem, hbm, vmem, vmem, hbm, smem, smem],
+        out_specs=(vmem, vmem, vmem, vmem),
+        scratch_shapes=[
+            pltpu.VMEM(w.shape, BF16),
+            pltpu.VMEM((requests, rows, width), BF16),
+            pltpu.VMEM((hosted, width), F32),
+            pltpu.VMEM((n_tok, packed, lanes), BF16),
+            pltpu.VMEM((n_tok, hosted, w.shape[0]), BF16),
+            pltpu.VMEM((n_tok * hosted, w.shape[0]), F32),
+            pltpu.VMEM((requests, positions, w.shape[0]), BF16),
+            pltpu.VMEM((hosted, w.shape[0]), F32),
+            pltpu.VMEM((2, requests, n_x, rows, width), BF16),
+            pltpu.VMEM((n_head, 1, width), BF16),
+            pltpu.VMEM((n_head, 1, width), BF16),
+            pltpu.VMEM((n_x, requests, rows, width), BF16),
+            pltpu.VMEM((n_x, requests, rows, width), BF16),
+            pltpu.VMEM((2, 2, rows, width), BF16),
+            pltpu.VMEM((2, requests, rows, width), BF16),
+            sem((4,)),
+            sem((n_tok,)),
+            sem((n_tok,)),
+            sem((n_tok,)),
+            sem((n_tok,)),
+            sem((n_head,)),
+            sem((n_head,)),
+            sem((ring,)),
+            sem((ring,)),
+        ],
+        compiler_params=pltpu.CompilerParams(
+            collective_id=3, has_side_effects=True, vmem_limit_bytes=56 * 1024 * 1024
+        ),
+        name="mix",
+    )(attn, dattn, states, dstates, gain, w, homes, dhomes)
+
+
 def shards(
     prefill_states,
     decode_states,
@@ -625,96 +1061,43 @@
 ):
     n_tok = lax.axis_size("tok")
     n_head = lax.axis_size("head")
-    my_tok = lax.axis_index("tok")
-    my_head = lax.axis_index("head")
-    requests, positions, width = prefill_states.shape
-    hosted = decode_states.shape[0]
-    heads_per = w_qkv.shape[2] // HD
-    stretch = positions * n_tok
-    units = requests * heads_per
-    features = heads_per * HD
-    normed_pre = rms_norm(prefill_states, attn_gain).reshape(requests * positions, width)
-    normed_dec = rms_norm(decode_states, attn_gain)
-    normed = jnp.concatenate([normed_pre, normed_dec], axis=0)
-    projected = jnp.dot(
-        normed, w_qkv.reshape(width, 3 * features), preferred_element_type=jnp.float32
-    ).astype(jnp.bfloat16)
-    proj_pre = projected[: requests * positions].reshape(requests, positions, 3, heads_per, HD)
-    proj_dec = projected[requests * positions :]
-    unit_ids = jnp.arange(units, dtype=jnp.int32)
-    host_ids = jnp.arange(n_tok, dtype=jnp.int32)
-    hosted_unit = jnp.sum(
-        jnp.where(prefill_home[None, :] == host_ids[:, None], unit_ids[None, :], 0), axis=1
+    width = prefill_states.shape[2]
+    arrived, arrived_dec = project(
+        prefill_states,
+        decode_states,
+        attn_gain.reshape(1, -1),
+        jnp.transpose(w_qkv, (1, 0, 2)),
+        prefill_home,
+        n_tok,
     )
-    by_unit = jnp.transpose(proj_pre, (0, 3, 1, 2, 4)).reshape(units, positions * 3 * HD)
-    outgoing = jnp.take(by_unit, hosted_unit, axis=0)
-    pre_cols = positions * 3 * HD
-    spread = jnp.broadcast_to(
-        proj_dec.reshape(1, hosted * 3 * features), (n_tok, hosted * 3 * features)
-    )
-    outgoing = jnp.concatenate([outgoing, spread], axis=1)
-    arrived = lax.all_to_all(outgoing, "tok", split_axis=0, concat_axis=0, tiled=True)
-    arrived_dec = arrived[:, pre_cols:].reshape(n_tok * hosted, 3, heads_per, HD)
-    arrived_pre = arrived[:, :pre_cols].reshape(stretch, 3, HD)
-    my_unit = hosted_unit[my_tok]
-    length = prefill_lengths[my_unit // heads_per]
-    slots = my_tok * hosted + jnp.arange(hosted, dtype=jnp.int32)
-    all_requests = jnp.arange(decode_home.shape[0], dtype=jnp.int32)
-    anchor = jnp.sum(
-        jnp.where(decode_home[None, :] == slots[:, None], all_requests[None, :], 0), axis=1
-    )
-    mine = jnp.take(arrived_dec, anchor, axis=0).reshape(hosted, 3 * features)
-    qkv = jnp.pad(arrived_pre.reshape(stretch, 3 * HD), ((0, 0), (0, HD)))
-    attn_unit, decode_attn = attention(
+    attn, dattn = attention(
         prefill_pages,
-        length.reshape(1),
+        prefill_lengths,
+        prefill_home,
         decode_pages,
         decode_lengths,
-        qkv,
-        mine,
+        decode_home,
+        arrived,
+        arrived_dec,
         prefill_pool.reshape(-1, 2 * HD),
         decode_pool.reshape(-1, decode_pool.shape[2]),
     )
-    backward = attn_unit.reshape(n_tok, positions * HD)
-    back_cols = positions * HD
-    spread_back = jnp.broadcast_to(
-        decode_attn.reshape(1, hosted * features), (n_tok, hosted * features)
+    normed, dnormed, resid, dresid = mix(
+        attn,
+        dattn,
+        prefill_states,
+        decode_states,
+        ffn_gain.reshape(1, -1),
+        w_out,
+        prefill_home,
+        decode_home,
+        n_head,
     )
-    backward = jnp.concatenate([backward, spread_back], axis=1)
-    returned = lax.all_to_all(backward, "tok", split_axis=0, concat_axis=0, tiled=True)
-    by_slot = returned[:, back_cols:].reshape(n_tok * hosted, features)
-    my_slots = lax.dynamic_slice_in_dim(decode_home, my_tok * hosted, hosted, 0)
-    attn_dec = jnp.take(by_slot, my_slots, axis=0)
-    attn_pre = jnp.take(returned[:, :back_cols], prefill_home, axis=0).reshape(
-        requests, heads_per, positions, HD
-    )
-    block_rows = positions // n_head
-    decode_share = hosted // n_head
-    per = requests * block_rows + decode_share
-    pre_rows = jnp.transpose(attn_pre, (0, 2, 1, 3)).reshape(requests, n_head, block_rows, features)
-    pre_rows = jnp.transpose(pre_rows, (1, 0, 2, 3)).reshape(
-        n_head, requests * block_rows, features
-    )
-    dec_rows = attn_dec.reshape(n_head, decode_share, features)
-    ordered = jnp.concatenate([pre_rows, dec_rows], axis=1).reshape(n_head * per, features)
-    mixed_rows = lax.psum_scatter(
-        jnp.dot(ordered, w_out, preferred_element_type=jnp.float32).astype(jnp.bfloat16),
-        "head",
-        scatter_dimension=0,
-        tiled=True,
-    ).astype(jnp.float32)
-    own_pre = lax.dynamic_slice_in_dim(prefill_states, my_head * block_rows, block_rows, 1).reshape(
-        requests * block_rows, width
-    )
-    own_dec = lax.dynamic_slice_in_dim(decode_states, my_head * decode_share, decode_share, 0)
-    resid = jnp.concatenate([own_pre, own_dec], axis=0).astype(jnp.float32) + mixed_rows
-    normed_mid = rms_norm(resid, ffn_gain)
-    rows = requests * block_rows
     prefill_out, decode_out = ffn(
-        normed_mid[:rows].reshape(-1, Q, width),
-        normed_mid[rows:],
-        resid[:rows].reshape(-1, Q, width),
-        resid[rows:],
+        normed,
+        dnormed,
+        resid,
+        dresid,
         jnp.transpose(w_gate_up, (1, 2, 0)).reshape(-1, width),
         w_down,
         n_tok,

time: 222 us -> 165 us (0.74); the launches traced: 218 us -> 164 us
  Pallas kernels: 104 us -> 161 us
  local copies, waits for them, and re-layouts: 42.8 us -> 2.97 us
  blocking collectives: 23.9 us -> 0 us
  waiting for transfers between devices: 20.1 us -> 0 us
  starting transfers between devices: 13.3 us -> 0 us
  other arithmetic: 6.98 us -> 0 us
  between operations: 4.38 us -> 0.66 us
  matrix products: 3.52 us -> 0 us
    pallas_call x1 -> x3, Pallas kernels: 40.5 us -> 93.8 us  [the longest x1 41.3 us: attention(): pl.pallas_call(attention_kernel, out_shape=(jax.ShapeDtypeStruct((n_tok,...]
    unnamed x1 -> x0, blocking collectives: 23.9 us -> none
    all_to_all x2 -> x0, waiting for transfers between devices: 19.2 us -> none  [the longest x1 11.4 us: shards(): lax.all_to_all(outgoing, 'tok', split_axis=0, concat_axis=0, tiled=True)]
    unnamed x35 -> x2, local copies, waits for them, and re-layouts: 21.8 us -> 2.97 us
    all_to_all x2 -> x0, starting transfers between devices: 11.8 us -> none  [the longest x1 8.21 us: shards(): lax.all_to_all(outgoing, 'tok', split_axis=0, concat_axis=0, tiled=True)]
    reshape x7 -> x0, local copies, waits for them, and re-layouts: 6.09 us -> none  [the longest x1 2.88 us: shards(): jnp.transpose(proj_pre, (0, 3, 1, 2, 4)).reshape(units, positions * 3 * HD)]
    pallas_call x1, Pallas kernels: 63 us -> 66.9 us  [ffn(): pl.pallas_call(ffn_kernel, out_shape=(jax.ShapeDtypeStruct(block.shape, B...]
    gather x6 -> x0, local copies, waits for them, and re-layouts: 3.55 us -> none  [the longest x2 1.25 us: shards(): jnp.take(returned[:, :back_cols], prefill_home, axis=0)]
  transfers between devices with their start and end apart: 3 -> 0, of which waited for: 3 -> 0; matrix products, arithmetic and copies ran while one was open for 1% -> 0% of each run, Pallas kernels for 0% -> 0%
where the time goes in v2:
time: 165 us; the launch traced here: 164 us
  Pallas kernels  161 us (98%)
  local copies, waits for them, and re-layouts  2.97 us (2%)
    pallas_call x1, Pallas kernels, ffn(): pl.pallas_call(ffn_kernel, out_shape=(jax.ShapeDtypeStruct(block.shape, B...  66.9 us
    pallas_call x1, Pallas kernels, attention(): pl.pallas_call(attention_kernel, out_shape=(jax.ShapeDtypeStruct((n_tok,...  41.3 us
    pallas_call x1, Pallas kernels, mix(): pl.pallas_call(mix_kernel, out_shape=(jax.ShapeDtypeStruct((requests, row...  28.8 us
    pallas_call x1, Pallas kernels, project(): pl.pallas_call(project_kernel, out_shape=(jax.ShapeDtypeStruct((n_tok, pa...  23.7 us

profile of v2, /device:TPU:0, one launch (start us, length us, event | category | flops | bytes accessed | tf_op | source)
XLA Modules:
  0.0 164.3 jit_solution(8887716427949062823)
XLA Ops:
  0.6 23.7 %project.1 = (bf16[16,192,128]{2,1,0:T(8,128)(2,1)}, bf16[16,8,768]{2,1,0:T(8,128)(2,1)}) custom-call(bf16[4,128,2048]{2,1,0:T(8,128)(2,1)} %states_hbm.1, bf16[8,2048]{1,0:T(8,128)(2,1)} %dstates.3, f32[1,2048]{1,0:T(1,128)} %bitcast.12, bf16[3,2048,256]{2,1,0:T(8,128)(2,1)} %bitcast.9, s32[16]{0:T(128)} %homes.5), custom_call_target="tpu_custom_call" | custom-call | tf_op jit(solution)/shard_map/project/pallas_call | solution.py:769
  24.4 41.3 %attention.1 = (bf16[16,64,128]{2,1,0:T(8,128)(2,1)}, bf16[8,256]{1,0:T(8,128)(2,1)}) custom-call(s32[1,48]{1,0:T(1,128)} %pages.1, s32[4]{0:T(128)} %lengths.1, s32[16]{0:T(128)} %homes.5, s32[8,32]{1,0:T(8,128)} %dpages.1, s32[8]{0:T(128)} %dlens.1, s32[128]{0:T(128)} %dhomes.3, bf16[16,192,128]{2,1,0:T(8,128)(2,1)} %get-tuple-element.10.arrived, ...), custom_call_target="tpu_custom_call" | custom-call | tf_op jit(solution)/shard_map/attention/pallas_call | solution.py:281
  65.7 28.8 %mix.1 = (bf16[4,16,2048]{2,1,0:T(8,128)(2,1)}, bf16[1,2048]{1,0:T(2,128)(2,1)}, f32[4,16,2048]{2,1,0:T(8,128)}, f32[1,2048]{1,0:T(1,128)}) custom-call(bf16[16,64,128]{2,1,0:T(8,128)(2,1)} %get-tuple-element.12.attn, bf16[8,256]{1,0:T(8,128)(2,1)} %get-tuple-element.13.dattn, bf16[4,128,2048]{2,1,0:T(8,128)(2,1)} %states_hbm.1, bf16[8,2048]{1,0:T(8,128)(2,1)} %dstates.3, ...), custom_call_target="tpu_custom_call" | custom-call | tf_op jit(solution)/shard_map/mix/pallas_call | solution.py:1001
  94.5 66.9 %ffn.1 = (bf16[4,16,2048]{2,1,0:T(8,128)(2,1)}, bf16[1,2048]{1,0:T(2,128)(2,1)}) custom-call(bf16[4,16,2048]{2,1,0:T(8,128)(2,1)} %get-tuple-element.14.block_ref, bf16[1,2048]{1,0:T(2,128)(2,1)} %get-tuple-element.15.drow_ref, f32[4,16,2048]{2,1,0:T(8,128)} %get-tuple-element.16.resid_ref, f32[1,2048]{1,0:T(1,128)} %get-tuple-element.17.dresid_ref, ...), custom_call_target="tpu_custom_call" | custom-call | tf_op jit(solution)/shard_map/ffn/pallas_call | solution.py:613
  161.3 1.7 %copy.20 = bf16[4,16,2048]{2,1,0:T(8,128)(2,1)} copy(bf16[4,16,2048]{2,1,0:T(8,128)(2,1)} %get-tuple-element.20) | data formatting | bytes 524288
  163.0 1.3 copy.21

commit v3 on v2

--- a/solution.py
+++ b/solution.py
@@ -168,7 +168,7 @@
         make_scores(0, c, False)
         return 0
 
-    lax.fori_loop(0, cached_chunks, first, 0)
+    lax.fori_loop(0, cached_chunks, first, 0, unroll=4)
     make_scores(0, cached_chunks, True)
     finish_top(0)
     for i in range(blocks):
@@ -182,7 +182,7 @@
                 mix(i, c)
                 return 0
 
-            lax.fori_loop(0, chunks, both, 0)
+            lax.fori_loop(0, chunks, both, 0, unroll=4)
             make_scores(i + 1, chunks, True)
             finish_top(i + 1)
         else:
@@ -191,7 +191,7 @@
                 mix(i, c)
                 return 0
 
-            lax.fori_loop(0, chunks, last, 0)
+            lax.fori_loop(0, chunks, last, 0, unroll=4)
         total = acc[...]
         result = pltpu.roll(total, HD, 1) / total
         for j in range(QB // PAGE):
@@ -457,19 +457,15 @@
         gate = both[:, :width]
         return (jax.nn.gelu(gate, approximate=True) * both[:, width:]).astype(BF16)
 
-    def compute(half, a2):
-        rows = x[half, a2].reshape(4 * 2 * Q, x.shape[-1])
+    def compute(a2):
+        rows = x[:, a2].reshape(2 * 4 * 2 * Q, x.shape[-1])
         result = jnp.dot(hidden_of(rows), wdown[...], preferred_element_type=F32)
-        part[half, a2] = result.astype(BF16).reshape(4, 2, Q, x.shape[-1])
+        part[:, a2] = result.astype(BF16).reshape(2, 4, 2, Q, x.shape[-1])
 
     load_gu.wait()
     load_down.wait()
 
-    def group0(i, _):
-        compute(i, 0)
-        return 0
-
-    lax.fori_loop(0, 2, group0, 0)
+    compute(0)
     for a1 in (3, 1):
         for half in range(2):
             wait(half, 3, a1)
@@ -481,10 +477,10 @@
         relay2(half, 2)
 
     def group13(i, _):
-        compute(i % 2, 3 - 2 * (i // 2))
+        compute(3 - 2 * i)
         return 0
 
-    lax.fori_loop(0, 4, group13, 0)
+    lax.fori_loop(0, 2, group13, 0)
     came = {}
     for half in range(2):
         came[half, 0, 1] = send(
@@ -519,7 +515,8 @@
     for half in range(2):
         for a1 in range(4):
             wait(half, 2, a1)
-        compute(half, 2)
+    compute(2)
+    for half in range(2):
         hop[half, 0] = send(part.at[half, 2, :, 0], relay.at[half, 0], axis2[half](1))
         hop[half, 1] = send(part.at[half, 2, :, 1], relay.at[half, 1], axis2[half](-1))
     for half in range(2):

time: 165 us -> 155 us (0.939)
  Pallas kernels: 161 us -> 151 us
    pallas_call x1, Pallas kernels: 41.3 us -> 32.9 us  [attention(): pl.pallas_call(attention_kernel, out_shape=(jax.ShapeDtypeStruct((n_tok,...]
    pallas_call x1, Pallas kernels: 66.9 us -> 65.1 us  [ffn(): pl.pallas_call(ffn_kernel, out_shape=(jax.ShapeDtypeStruct(block.shape, B...]
where the time goes in v3:
time: 155 us; the launch traced here: 154 us
  Pallas kernels  151 us (97%)
  local copies, waits for them, and re-layouts  2.97 us (2%)
    pallas_call x1, Pallas kernels, ffn(): pl.pallas_call(ffn_kernel, out_shape=(jax.ShapeDtypeStruct(block.shape, B...  65.1 us
    pallas_call x1, Pallas kernels, attention(): pl.pallas_call(attention_kernel, out_shape=(jax.ShapeDtypeStruct((n_tok,...  32.9 us
    pallas_call x1, Pallas kernels, mix(): pl.pallas_call(mix_kernel, out_shape=(jax.ShapeDtypeStruct((requests, row...  28.9 us
    pallas_call x1, Pallas kernels, project(): pl.pallas_call(project_kernel, out_shape=(jax.ShapeDtypeStruct((n_tok, pa...  23.7 us

profile of v3, /device:TPU:0, one launch (start us, length us, event | category | flops | bytes accessed | tf_op | source)
XLA Modules:
  0.0 154.2 jit_solution(15913946644222603012)
XLA Ops:
  0.6 23.7 %project.1 = (bf16[16,192,128]{2,1,0:T(8,128)(2,1)}, bf16[16,8,768]{2,1,0:T(8,128)(2,1)}) custom-call(bf16[4,128,2048]{2,1,0:T(8,128)(2,1)} %states_hbm.1, bf16[8,2048]{1,0:T(8,128)(2,1)} %dstates.3, f32[1,2048]{1,0:T(1,128)} %bitcast.12, bf16[3,2048,256]{2,1,0:T(8,128)(2,1)} %bitcast.9, s32[16]{0:T(128)} %homes.5), custom_call_target="tpu_custom_call" | custom-call | tf_op jit(solution)/shard_map/project/pallas_call | solution.py:766
  24.4 32.9 %attention.1 = (bf16[16,64,128]{2,1,0:T(8,128)(2,1)}, bf16[8,256]{1,0:T(8,128)(2,1)}) custom-call(s32[1,48]{1,0:T(1,128)} %pages.1, s32[4]{0:T(128)} %lengths.1, s32[16]{0:T(128)} %homes.5, s32[8,32]{1,0:T(8,128)} %dpages.1, s32[8]{0:T(128)} %dlens.1, s32[128]{0:T(128)} %dhomes.3, bf16[16,192,128]{2,1,0:T(8,128)(2,1)} %get-tuple-element.10.arrived, ...), custom_call_target="tpu_custom_call" | custom-call | tf_op jit(solution)/shard_map/attention/pallas_call | solution.py:281
  57.2 28.9 %mix.1 = (bf16[4,16,2048]{2,1,0:T(8,128)(2,1)}, bf16[1,2048]{1,0:T(2,128)(2,1)}, f32[4,16,2048]{2,1,0:T(8,128)}, f32[1,2048]{1,0:T(1,128)}) custom-call(bf16[16,64,128]{2,1,0:T(8,128)(2,1)} %get-tuple-element.12.attn, bf16[8,256]{1,0:T(8,128)(2,1)} %get-tuple-element.13.dattn, bf16[4,128,2048]{2,1,0:T(8,128)(2,1)} %states_hbm.1, bf16[8,2048]{1,0:T(8,128)(2,1)} %dstates.3, ...), custom_call_target="tpu_custom_call" | custom-call | tf_op jit(solution)/shard_map/mix/pallas_call | solution.py:998
  86.1 65.1 %ffn.1 = (bf16[4,16,2048]{2,1,0:T(8,128)(2,1)}, bf16[1,2048]{1,0:T(2,128)(2,1)}) custom-call(bf16[4,16,2048]{2,1,0:T(8,128)(2,1)} %get-tuple-element.14.block_ref, bf16[1,2048]{1,0:T(2,128)(2,1)} %get-tuple-element.15.drow_ref, f32[4,16,2048]{2,1,0:T(8,128)} %get-tuple-element.16.resid_ref, f32[1,2048]{1,0:T(1,128)} %get-tuple-element.17.dresid_ref, ...), custom_call_target="tpu_custom_call" | custom-call | tf_op jit(solution)/shard_map/ffn/pallas_call | solution.py:610
  151.2 1.7 %copy.20 = bf16[4,16,2048]{2,1,0:T(8,128)(2,1)} copy(bf16[4,16,2048]{2,1,0:T(8,128)(2,1)} %get-tuple-element.20) | data formatting | bytes 524288
  152.9 1.3 copy.21

commit v4 on v3

--- a/solution.py
+++ b/solution.py
@@ -110,7 +110,7 @@
         vals[where_at, :] = jnp.where(lane < HD, 1.0, page).astype(BF16)
         return 0
 
-    lax.fori_loop(0, npages, fill_cached, 0)
+    lax.fori_loop(0, npages, fill_cached, 0, unroll=4)
 
     half = PAGE // 2
 
@@ -129,7 +129,7 @@
         query[at_high, :] = high.astype(BF16)
         return 0
 
-    lax.fori_loop(0, stretch // PAGE, fill_own, 0)
+    lax.fori_loop(0, stretch // PAGE, fill_own, 0, unroll=4)
 
     def fold(s):
         best = s[:, :PAGE]
@@ -516,24 +516,31 @@
         for a1 in range(4):
             wait(half, 2, a1)
     compute(2)
-    for half in range(2):
-        hop[half, 0] = send(part.at[half, 2, :, 0], relay.at[half, 0], axis2[half](1))
-        hop[half, 1] = send(part.at[half, 2, :, 1], relay.at[half, 1], axis2[half](-1))
-    for half in range(2):
-        hop[half, 0].wait_recv()
-        part[half, 1, :, 0] = (
-            part[half, 1, :, 0].astype(F32) + relay[half, 0].astype(F32)
-        ).astype(BF16)
-        came[half, 0, 0] = send(
-            part.at[half, 1, :, 0], direct.at[half, 0, :, 0], axis2[half](1)
-        )
-        hop[half, 1].wait_recv()
-        part[half, 3, :, 1] = (
-            part[half, 3, :, 1].astype(F32) + relay[half, 1].astype(F32)
-        ).astype(BF16)
-        came[half, 1, 1] = send(
-            part.at[half, 3, :, 1], direct.at[half, 1, :, 1], axis2[half](-1)
-        )
+    order = (2, 1, 3, 0)
+    for a1 in order:
+        for half in range(2):
+            hop[half, 0, a1] = send(
+                part.at[half, 2, a1, 0], relay.at[half, 0, a1], axis2[half](1)
+            )
+            hop[half, 1, a1] = send(
+                part.at[half, 2, a1, 1], relay.at[half, 1, a1], axis2[half](-1)
+            )
+    for a1 in order:
+        for half in range(2):
+            hop[half, 0, a1].wait_recv()
+            part[half, 1, a1, 0] = (
+                part[half, 1, a1, 0].astype(F32) + relay[half, 0, a1].astype(F32)
+            ).astype(BF16)
+            came[half, 0, 0, a1] = send(
+                part.at[half, 1, a1, 0], direct.at[half, 0, a1, 0], axis2[half](1)
+            )
+            hop[half, 1, a1].wait_recv()
+            part[half, 3, a1, 1] = (
+                part[half, 3, a1, 1].astype(F32) + relay[half, 1, a1].astype(F32)
+            ).astype(BF16)
+            came[half, 1, 1, a1] = send(
+                part.at[half, 3, a1, 1], direct.at[half, 1, a1, 1], axis2[half](-1)
+            )
     dtotal = dresid_ref[...] + pdec[0].astype(F32)
     for c in dec_back:
         c.wait_recv()
@@ -542,35 +549,36 @@
     dout_ref[...] = dtotal.astype(BF16)
     hop1 = {}
     came1 = {}
-    for half in range(2):
-        for side in range(2):
-            for q in range(2):
-                came[half, side, q].wait_recv()
-        for a1 in (2, 1, 3, 0):
-            total = (
-                part[half, 0, a1].astype(F32)
-                + direct[half, 0, a1].astype(F32)
-                + direct[half, 1, a1].astype(F32)
-            )
-            if a1 == 0:
-                first[half] = total
-            else:
-                sums[half, a1] = total.astype(BF16)
-            if a1 == 2:
-                hop1[half, 0] = send(
-                    sums.at[half, 2, 0], relay1.at[half, 0], axis1[half](1)
-                )
-                hop1[half, 1] = send(
-                    sums.at[half, 2, 1], relay1.at[half, 1], axis1[half](-1)
-                )
-            if a1 == 1:
-                came1[half, 0, 1] = send(
-                    sums.at[half, 1, 1], direct1.at[half, 0, 1], axis1[half](1)
-                )
-            if a1 == 3:
-                came1[half, 1, 0] = send(
-                    sums.at[half, 3, 0], direct1.at[half, 1, 0], axis1[half](-1)
-                )
+
+    def collect(half, a1):
+        came[half, 0, 0, a1].wait_recv()
+        came[half, 1, 1, a1].wait_recv()
+        total = (
+            part[half, 0, a1].astype(F32)
+            + direct[half, 0, a1].astype(F32)
+            + direct[half, 1, a1].astype(F32)
+        )
+        if a1 == 0:
+            first[half] = total
+        else:
+            sums[half, a1] = total.astype(BF16)
+
+    for half in range(2):
+        came[half, 0, 1].wait_recv()
+        came[half, 1, 0].wait_recv()
+        collect(half, 2)
+        hop1[half, 0] = send(sums.at[half, 2, 0], relay1.at[half, 0], axis1[half](1))
+        hop1[half, 1] = send(sums.at[half, 2, 1], relay1.at[half, 1], axis1[half](-1))
+    for half in range(2):
+        collect(half, 1)
+        came1[half, 0, 1] = send(
+            sums.at[half, 1, 1], direct1.at[half, 0, 1], axis1[half](1)
+        )
+    for half in range(2):
+        collect(half, 3)
+        came1[half, 1, 0] = send(
+            sums.at[half, 3, 0], direct1.at[half, 1, 0], axis1[half](-1)
+        )
     for half in range(2):
         hop1[half, 0].wait_recv()
         sums[half, 1, 0] = (
@@ -586,6 +594,8 @@
         came1[half, 1, 1] = send(
             sums.at[half, 3, 1], direct1.at[half, 1, 1], axis1[half](-1)
         )
+    for half in range(2):
+        collect(half, 0)
     for half in range(2):
         for side in range(2):
             for q in range(2):
@@ -600,7 +610,7 @@
         c.wait_send()
 
 
-FFN_SENDS = 2 * (2 + 2 + 8 + 8 + 6 + 6)
+FFN_SENDS = 2 * (2 + 2 + 8 + 8 + 2 + 16 + 6)
 
 
 def ffn(block, drow, resid, dresid, wgu, wdown, n_tok):
@@ -954,18 +964,20 @@
         else:
             sums[dx] = total.astype(BF16)
         if dx == 2:
-            hop[0] = send(sums.at[2, 0:2], relay.at[0], up)
-            hop[1] = send(sums.at[2, 2:4], relay.at[1], down)
+            for i in range(2):
+                hop[0, i] = send(sums.at[2, i], relay.at[0, i], up)
+                hop[1, i] = send(sums.at[2, 2 + i], relay.at[1, i], down)
         if dx == 1:
             came[0, 1] = send(sums.at[1, 2:4], direct.at[0, 2:4], up)
         if dx == 3:
             came[1, 0] = send(sums.at[3, 0:2], direct.at[1, 0:2], down)
-    hop[0].wait_recv()
-    sums[1, 0:2] = (sums[1, 0:2].astype(F32) + relay[0].astype(F32)).astype(BF16)
-    came[0, 0] = send(sums.at[1, 0:2], direct.at[0, 0:2], up)
-    hop[1].wait_recv()
-    sums[3, 2:4] = (sums[3, 2:4].astype(F32) + relay[1].astype(F32)).astype(BF16)
-    came[1, 1] = send(sums.at[3, 2:4], direct.at[1, 2:4], down)
+    for i in range(2):
+        hop[0, i].wait_recv()
+        sums[1, i] = (sums[1, i].astype(F32) + relay[0, i].astype(F32)).astype(BF16)
+        came[0, 0, i] = send(sums.at[1, i], direct.at[0, i], up)
+        hop[1, i].wait_recv()
+        sums[3, 2 + i] = (sums[3, 2 + i].astype(F32) + relay[1, i].astype(F32)).astype(BF16)
+        came[1, 1, i] = send(sums.at[3, 2 + i], direct.at[1, 2 + i], down)
     gain = gain_ref[...]
     dtotal = drows[pl.ds(head, 1), :] + pdec[head].astype(F32)
     for c in sends[2 * (n_tok - 1) :]:
@@ -994,7 +1006,7 @@
     smem = pl.BlockSpec(memory_space=pltpu.SMEM)
     hbm = pl.BlockSpec(memory_space=pl.ANY)
     sem = pltpu.SemaphoreType.DMA
-    ring = 4 + 6
+    ring = 4 + 4 + 2 + 4
     return pl.pallas_call(
         mix_kernel,
         out_shape=(
@@ -1036,6 +1048,22 @@
         ),
         name="mix",
     )(attn, dattn, states, dstates, gain, w, homes, dhomes)
+
+
+def keep_kernel(left, right, left_out, right_out):
+    left_out[...] = left[...]
+    right_out[...] = right[...]
+
+
+def keep(left, right):
+    vmem = pl.BlockSpec(memory_space=pltpu.VMEM)
+    return pl.pallas_call(
+        keep_kernel,
+        out_shape=tuple(jax.ShapeDtypeStruct(a.shape, a.dtype) for a in (left, right)),
+        in_specs=[vmem, vmem],
+        out_specs=(vmem, vmem),
+        name="keep",
+    )(left, right)
 
 
 def shards(
@@ -1099,7 +1127,7 @@
         w_down,
         n_tok,
     )
-    return (prefill_out, decode_out)
+    return keep(prefill_out, decode_out)
 
 
 def solution(mesh):

time: 155 us -> 148 us (0.955)
  Pallas kernels: 151 us -> 147 us
  local copies, waits for them, and re-layouts: 2.97 us -> 0 us
    pallas_call x1, Pallas kernels: 65.1 us -> 60.3 us  [ffn(): pl.pallas_call(ffn_kernel, out_shape=(jax.ShapeDtypeStruct(block.shape, B...]
    unnamed x2 -> x0, local copies, waits for them, and re-layouts: 2.97 us -> none
    pallas_call x0 -> x1, Pallas kernels: none -> 1.68 us  [keep(): pl.pallas_call(keep_kernel, out_shape=tuple((jax.ShapeDtypeStruct(a.shape...]
where the time goes in v4:
time: 148 us
  Pallas kernels  147 us (99%)
    pallas_call x1, Pallas kernels, ffn(): pl.pallas_call(ffn_kernel, out_shape=(jax.ShapeDtypeStruct(block.shape, B...  60.3 us
    pallas_call x1, Pallas kernels, attention(): pl.pallas_call(attention_kernel, out_shape=(jax.ShapeDtypeStruct((n_tok,...  32.6 us
    pallas_call x1, Pallas kernels, mix(): pl.pallas_call(mix_kernel, out_shape=(jax.ShapeDtypeStruct((requests, row...  29 us
    pallas_call x1, Pallas kernels, project(): pl.pallas_call(project_kernel, out_shape=(jax.ShapeDtypeStruct((n_tok, pa...  23.7 us

profile of v4, /device:TPU:0, one launch (start us, length us, event | category | flops | bytes accessed | tf_op | source)
XLA Modules:
  0.0 148.0 jit_solution(968575822463985303)
XLA Ops:
  0.6 23.7 %project.1 = (bf16[16,192,128]{2,1,0:T(8,128)(2,1)}, bf16[16,8,768]{2,1,0:T(8,128)(2,1)}) custom-call(bf16[4,128,2048]{2,1,0:T(8,128)(2,1)} %states_hbm.1, bf16[8,2048]{1,0:T(8,128)(2,1)} %dstates.3, f32[1,2048]{1,0:T(1,128)} %bitcast.12, bf16[3,2048,256]{2,1,0:T(8,128)(2,1)} %bitcast.9, s32[16]{0:T(128)} %homes.5), custom_call_target="tpu_custom_call" | custom-call | tf_op jit(solution)/shard_map/project/pallas_call | solution.py:776
  24.4 32.6 %attention.1 = (bf16[16,64,128]{2,1,0:T(8,128)(2,1)}, bf16[8,256]{1,0:T(8,128)(2,1)}) custom-call(s32[1,48]{1,0:T(1,128)} %pages.1, s32[4]{0:T(128)} %lengths.1, s32[16]{0:T(128)} %homes.5, s32[8,32]{1,0:T(8,128)} %dpages.1, s32[8]{0:T(128)} %dlens.1, s32[128]{0:T(128)} %dhomes.3, bf16[16,192,128]{2,1,0:T(8,128)(2,1)} %get-tuple-element.12.arrived, ...), custom_call_target="tpu_custom_call" | custom-call | tf_op jit(solution)/shard_map/attention/pallas_call | solution.py:281
  57.0 29.0 %mix.1 = (bf16[4,16,2048]{2,1,0:T(8,128)(2,1)}, bf16[1,2048]{1,0:T(2,128)(2,1)}, f32[4,16,2048]{2,1,0:T(8,128)}, f32[1,2048]{1,0:T(1,128)}) custom-call(bf16[16,64,128]{2,1,0:T(8,128)(2,1)} %get-tuple-element.14.attn, bf16[8,256]{1,0:T(8,128)(2,1)} %get-tuple-element.15.dattn, bf16[4,128,2048]{2,1,0:T(8,128)(2,1)} %states_hbm.1, bf16[8,2048]{1,0:T(8,128)(2,1)} %dstates.3, ...), custom_call_target="tpu_custom_call" | custom-call | tf_op jit(solution)/shard_map/mix/pallas_call | solution.py:1010
  86.0 60.3 %ffn.1 = (bf16[4,16,2048]{2,1,0:T(8,128)(2,1)}, bf16[1,2048]{1,0:T(2,128)(2,1)}) custom-call(bf16[4,16,2048]{2,1,0:T(8,128)(2,1)} %get-tuple-element.16.block_ref, bf16[1,2048]{1,0:T(2,128)(2,1)} %get-tuple-element.17.drow_ref, f32[4,16,2048]{2,1,0:T(8,128)} %get-tuple-element.18.resid_ref, f32[1,2048]{1,0:T(1,128)} %get-tuple-element.19.dresid_ref, ...), custom_call_target="tpu_custom_call" | custom-call | tf_op jit(solution)/shard_map/ffn/pallas_call | solution.py:620
  146.3 1.7 %keep.1 = (bf16[4,16,2048]{2,1,0:T(8,128)(2,1)}, bf16[1,2048]{1,0:T(2,128)(2,1)}) custom-call(bf16[4,16,2048]{2,1,0:T(8,128)(2,1)} %get-tuple-element.20.left, bf16[1,2048]{1,0:T(2,128)(2,1)} %get-tuple-element.21.right), custom_call_target="tpu_custom_call" | custom-call | tf_op jit(solution)/shard_map/keep/pallas_call | solution.py:1060

commit v5 on v4

--- a/solution.py
+++ b/solution.py
@@ -476,19 +476,13 @@
         wait(half, 1, 2)
         relay2(half, 2)
 
-    def group13(i, _):
-        compute(3 - 2 * i)
-        return 0
-
-    lax.fori_loop(0, 2, group13, 0)
     came = {}
-    for half in range(2):
-        came[half, 0, 1] = send(
-            part.at[half, 1, :, 1], direct.at[half, 0, :, 1], axis2[half](1)
-        )
-        came[half, 1, 0] = send(
-            part.at[half, 3, :, 0], direct.at[half, 1, :, 0], axis2[half](-1)
-        )
+    for a2, side, q, step in ((1, 0, 1, 1), (3, 1, 0, -1)):
+        compute(a2)
+        for half in range(2):
+            came[half, side, q] = send(
+                part.at[half, a2, :, q], direct.at[half, side, :, q], axis2[half](step)
+            )
     for c in dec_copies:
         c.wait_recv()
     for t in range(n_tok):

time: 148 us -> 148 us (level)
  no operation moved by 1% of the time
where the time goes in v5:
time: 148 us; the launch traced here: 147 us
  Pallas kernels  147 us (99%)
    pallas_call x1, Pallas kernels, ffn(): pl.pallas_call(ffn_kernel, out_shape=(jax.ShapeDtypeStruct(block.shape, B...  59.5 us
    pallas_call x1, Pallas kernels, attention(): pl.pallas_call(attention_kernel, out_shape=(jax.ShapeDtypeStruct((n_tok,...  32.7 us
    pallas_call x1, Pallas kernels, mix(): pl.pallas_call(mix_kernel, out_shape=(jax.ShapeDtypeStruct((requests, row...  29.1 us
    pallas_call x1, Pallas kernels, project(): pl.pallas_call(project_kernel, out_shape=(jax.ShapeDtypeStruct((n_tok, pa...  23.7 us

profile of v5, /device:TPU:0, one launch (start us, length us, event | category | flops | bytes accessed | tf_op | source)
XLA Modules:
  0.0 147.3 jit_solution(8106221376486243427)
XLA Ops:
  0.6 23.7 %project.1 = (bf16[16,192,128]{2,1,0:T(8,128)(2,1)}, bf16[16,8,768]{2,1,0:T(8,128)(2,1)}) custom-call(bf16[4,128,2048]{2,1,0:T(8,128)(2,1)} %states_hbm.1, bf16[8,2048]{1,0:T(8,128)(2,1)} %dstates.3, f32[1,2048]{1,0:T(1,128)} %bitcast.12, bf16[3,2048,256]{2,1,0:T(8,128)(2,1)} %bitcast.9, s32[16]{0:T(128)} %homes.5), custom_call_target="tpu_custom_call" | custom-call | tf_op jit(solution)/shard_map/project/pallas_call | solution.py:770
  24.4 32.7 %attention.1 = (bf16[16,64,128]{2,1,0:T(8,128)(2,1)}, bf16[8,256]{1,0:T(8,128)(2,1)}) custom-call(s32[1,48]{1,0:T(1,128)} %pages.1, s32[4]{0:T(128)} %lengths.1, s32[16]{0:T(128)} %homes.5, s32[8,32]{1,0:T(8,128)} %dpages.1, s32[8]{0:T(128)} %dlens.1, s32[128]{0:T(128)} %dhomes.3, bf16[16,192,128]{2,1,0:T(8,128)(2,1)} %get-tuple-element.12.arrived, ...), custom_call_target="tpu_custom_call" | custom-call | tf_op jit(solution)/shard_map/attention/pallas_call | solution.py:281
  57.1 29.1 %mix.1 = (bf16[4,16,2048]{2,1,0:T(8,128)(2,1)}, bf16[1,2048]{1,0:T(2,128)(2,1)}, f32[4,16,2048]{2,1,0:T(8,128)}, f32[1,2048]{1,0:T(1,128)}) custom-call(bf16[16,64,128]{2,1,0:T(8,128)(2,1)} %get-tuple-element.14.attn, bf16[8,256]{1,0:T(8,128)(2,1)} %get-tuple-element.15.dattn, bf16[4,128,2048]{2,1,0:T(8,128)(2,1)} %states_hbm.1, bf16[8,2048]{1,0:T(8,128)(2,1)} %dstates.3, ...), custom_call_target="tpu_custom_call" | custom-call | tf_op jit(solution)/shard_map/mix/pallas_call | solution.py:1004
  86.1 59.5 %ffn.1 = (bf16[4,16,2048]{2,1,0:T(8,128)(2,1)}, bf16[1,2048]{1,0:T(2,128)(2,1)}) custom-call(bf16[4,16,2048]{2,1,0:T(8,128)(2,1)} %get-tuple-element.16.block_ref, bf16[1,2048]{1,0:T(2,128)(2,1)} %get-tuple-element.17.drow_ref, f32[4,16,2048]{2,1,0:T(8,128)} %get-tuple-element.18.resid_ref, f32[1,2048]{1,0:T(1,128)} %get-tuple-element.19.dresid_ref, ...), custom_call_target="tpu_custom_call" | custom-call | tf_op jit(solution)/shard_map/ffn/pallas_call | solution.py:614
  145.6 1.7 %keep.1 = (bf16[4,16,2048]{2,1,0:T(8,128)(2,1)}, bf16[1,2048]{1,0:T(2,128)(2,1)}) custom-call(bf16[4,16,2048]{2,1,0:T(8,128)(2,1)} %get-tuple-element.20.left, bf16[1,2048]{1,0:T(2,128)(2,1)} %get-tuple-element.21.right), custom_call_target="tpu_custom_call" | custom-call | tf_op jit(solution)/shard_map/keep/pallas_call | solution.py:1054

commit v6 on v5

--- a/solution.py
+++ b/solution.py
@@ -711,25 +711,31 @@
         copy.start()
         copies.append(copy)
 
-    def project(r, _):
-        rows = normed[pl.ds(r * (positions // strip), positions // strip)].reshape(
-            positions, width
-        )
-        q, k, v = (jnp.dot(rows, w[i], preferred_element_type=F32) for i in range(3))
-        for j in range(per):
-            at = j // 2 * PAGE
-            qb, kb, vb = (a[:, at : at + PAGE] for a in (q, k, v))
-            if j % 2 == 0:
-                both = jnp.where(lane < HD, kb, pltpu.roll(vb, HD, 1))
-                pair = jnp.where(lane[:half] < HD, qb[:half], pltpu.roll(qb[half:], HD, 1))
-            else:
-                both = jnp.where(lane < HD, pltpu.roll(kb, HD, 1), vb)
-                pair = jnp.where(lane[:half] < HD, pltpu.roll(qb[:half], HD, 1), qb[half:])
-            units[r * per + j, :positions, :] = both.astype(BF16)
-            units[r * per + j, positions:, :] = pair.astype(BF16)
+    group = 2
+    strips = group * positions // strip
+
+    def project(g, _):
+        rows = normed[pl.ds(g * strips, strips)].reshape(group * positions, width)
+        full = [jnp.dot(rows, w[i], preferred_element_type=F32) for i in range(3)]
+        for m in range(group):
+            q, k, v = (a[m * positions : (m + 1) * positions] for a in full)
+            for j in range(per):
+                at = j // 2 * PAGE
+                qb, kb, vb = (a[:, at : at + PAGE] for a in (q, k, v))
+                if j % 2 == 0:
+                    both = jnp.where(lane < HD, kb, pltpu.roll(vb, HD, 1))
+                    turned = pltpu.roll(qb[half:], HD, 1)
+                    pair = jnp.where(lane[:half] < HD, qb[:half], turned)
+                else:
+                    both = jnp.where(lane < HD, pltpu.roll(kb, HD, 1), vb)
+                    turned = pltpu.roll(qb[:half], HD, 1)
+                    pair = jnp.where(lane[:half] < HD, turned, qb[half:])
+                unit = (g * group + m) * per + j
+                units[unit, :positions, :] = both.astype(BF16)
+                units[unit, positions:, :] = pair.astype(BF16)
         return 0
 
-    lax.fori_loop(0, requests, project, 0)
+    lax.fori_loop(0, requests // group, project, 0)
     for off in range(n_tok):
         target = (me + off) % n_tok
         unit = jnp.int32(0)
@@ -900,13 +906,6 @@
     for i in range(hosted):
         dleft[i : i + 1, :] = gdec_rows[pl.ds(dhomes[me * hosted + i], 1), :]
 
-    def project(r, _):
-        result = jnp.dot(left[r], w[...], preferred_element_type=F32).astype(BF16)
-        for k in range(n_head):
-            part[k % 2, r, k // 2] = result[k * rows : (k + 1) * rows]
-        return 0
-
-    lax.fori_loop(0, requests, project, 0)
     used = [0]
     ring = []
 
@@ -929,11 +928,12 @@
     up = (my_x + 1) % n_x * 2 + core
     down = (my_x + n_x - 1) % n_x * 2 + core
     order = (2, 1, 3, 0)
-    paired = {}
-    for dx in order:
-        paired[dx] = send(
-            part.at[1 - core, :, (my_x + dx) % n_x], pair.at[dx], partner
-        )
+    paired = []
+    for r in range(requests):
+        result = jnp.dot(left[r], w[...], preferred_element_type=F32).astype(BF16)
+        for k in range(n_head):
+            part[k % 2, r, k // 2] = result[k * rows : (k + 1) * rows]
+        paired.append(send(part.at[1 - core, r], pair.at[r], partner))
     dresult = jnp.dot(dleft[...].astype(BF16), w[...], preferred_element_type=F32)
     for k in range(n_head):
         pdec[k] = dresult[k : k + 1, :].astype(BF16)
@@ -951,8 +951,10 @@
     hop = {}
     came = {}
     for dx in order:
-        paired[dx].wait_recv()
-        total = part[core, :, (my_x + dx) % n_x].astype(F32) + pair[dx].astype(F32)
+        for c in paired if dx == order[0] else ():
+            c.wait_recv()
+        there = (my_x + dx) % n_x
+        total = part[core, :, there].astype(F32) + pair[:, there].astype(F32)
         if dx == 0:
             resid_ref[...] = total + own[...].astype(F32)
         else:
@@ -1023,7 +1025,7 @@
             pltpu.VMEM((2, requests, n_x, rows, width), BF16),
             pltpu.VMEM((n_head, 1, width), BF16),
             pltpu.VMEM((n_head, 1, width), BF16),
-            pltpu.VMEM((n_x, requests, rows, width), BF16),
+            pltpu.VMEM((requests, n_x, rows, width), BF16),
             pltpu.VMEM((n_x, requests, rows, width), BF16),
             pltpu.VMEM((2, 2, rows, width), BF16),
             pltpu.VMEM((2, requests, rows, width), BF16),

time: 148 us -> 147 us (level)
  no operation moved by 1% of the time
where the time goes in v6:
time: 147 us
  Pallas kernels  146 us (99%)
    pallas_call x1, Pallas kernels, ffn(): pl.pallas_call(ffn_kernel, out_shape=(jax.ShapeDtypeStruct(block.shape, B...  59.6 us
    pallas_call x1, Pallas kernels, attention(): pl.pallas_call(attention_kernel, out_shape=(jax.ShapeDtypeStruct((n_tok,...  32.8 us
    pallas_call x1, Pallas kernels, mix(): pl.pallas_call(mix_kernel, out_shape=(jax.ShapeDtypeStruct((requests, row...  28.6 us
    pallas_call x1, Pallas kernels, project(): pl.pallas_call(project_kernel, out_shape=(jax.ShapeDtypeStruct((n_tok, pa...  23.3 us

profile of v6, /device:TPU:0, one launch (start us, length us, event | category | flops | bytes accessed | tf_op | source)
XLA Modules:
  0.0 146.6 jit_solution(14395582254301428739)
XLA Ops:
  0.6 23.3 %project.1 = (bf16[16,192,128]{2,1,0:T(8,128)(2,1)}, bf16[16,8,768]{2,1,0:T(8,128)(2,1)}) custom-call(bf16[4,128,2048]{2,1,0:T(8,128)(2,1)} %states_hbm.1, bf16[8,2048]{1,0:T(8,128)(2,1)} %dstates.3, f32[1,2048]{1,0:T(1,128)} %bitcast.12, bf16[3,2048,256]{2,1,0:T(8,128)(2,1)} %bitcast.9, s32[16]{0:T(128)} %homes.5), custom_call_target="tpu_custom_call" | custom-call | tf_op jit(solution)/shard_map/project/pallas_call | solution.py:776
  23.9 32.8 %attention.1 = (bf16[16,64,128]{2,1,0:T(8,128)(2,1)}, bf16[8,256]{1,0:T(8,128)(2,1)}) custom-call(s32[1,48]{1,0:T(1,128)} %pages.1, s32[4]{0:T(128)} %lengths.1, s32[16]{0:T(128)} %homes.5, s32[8,32]{1,0:T(8,128)} %dpages.1, s32[8]{0:T(128)} %dlens.1, s32[128]{0:T(128)} %dhomes.3, bf16[16,192,128]{2,1,0:T(8,128)(2,1)} %get-tuple-element.12.arrived, ...), custom_call_target="tpu_custom_call" | custom-call | tf_op jit(solution)/shard_map/attention/pallas_call | solution.py:281
  56.7 28.6 %mix.1 = (bf16[4,16,2048]{2,1,0:T(8,128)(2,1)}, bf16[1,2048]{1,0:T(2,128)(2,1)}, f32[4,16,2048]{2,1,0:T(8,128)}, f32[1,2048]{1,0:T(1,128)}) custom-call(bf16[16,64,128]{2,1,0:T(8,128)(2,1)} %get-tuple-element.14.attn, bf16[8,256]{1,0:T(8,128)(2,1)} %get-tuple-element.15.dattn, bf16[4,128,2048]{2,1,0:T(8,128)(2,1)} %states_hbm.1, bf16[8,2048]{1,0:T(8,128)(2,1)} %dstates.3, ...), custom_call_target="tpu_custom_call" | custom-call | tf_op jit(solution)/shard_map/mix/pallas_call | solution.py:1006
  85.3 59.6 %ffn.1 = (bf16[4,16,2048]{2,1,0:T(8,128)(2,1)}, bf16[1,2048]{1,0:T(2,128)(2,1)}) custom-call(bf16[4,16,2048]{2,1,0:T(8,128)(2,1)} %get-tuple-element.16.block_ref, bf16[1,2048]{1,0:T(2,128)(2,1)} %get-tuple-element.17.drow_ref, f32[4,16,2048]{2,1,0:T(8,128)} %get-tuple-element.18.resid_ref, f32[1,2048]{1,0:T(1,128)} %get-tuple-element.19.dresid_ref, ...), custom_call_target="tpu_custom_call" | custom-call | tf_op jit(solution)/shard_map/ffn/pallas_call | solution.py:614
  144.9 1.7 %keep.1 = (bf16[4,16,2048]{2,1,0:T(8,128)(2,1)}, bf16[1,2048]{1,0:T(2,128)(2,1)}) custom-call(bf16[4,16,2048]{2,1,0:T(8,128)(2,1)} %get-tuple-element.20.left, bf16[1,2048]{1,0:T(2,128)(2,1)} %get-tuple-element.21.right), custom_call_target="tpu_custom_call" | custom-call | tf_op jit(solution)/shard_map/keep/pallas_call | solution.py:1056
